TPU v7x, 32 devices: a whole 2x2x4 slice. The times are simulated.
32 devices in a mesh: seq: 8 (over y, x, core), head: 4 (over z).
Axes of the slice: x: 2, y: 2, z: 4, core: 2. Of those that a mesh axis runs over, the one named last changes fastest.
Arguments:
- ssm_input: bfloat16 [1536, 16384], P('seq', 'head'), may hold values from -6 to 6
- state_in: bfloat16 [1536, 2048], P('seq'), may hold values from -0.375 to 0.375
- state_out: bfloat16 [1536, 2048], P('seq'), may hold values from -0.15625 to 0.15625
- step_size: float32 [1536, 256], P('seq', 'head'), may hold values from 0.5 to 1.5
- decay_rate: float32 [256], P('head'), may hold values from 3.25520833e-05 to 0.04
- forget: float32 [1536], P('seq'), may hold values from 0 to 0.9
- skip_gain: float32 [256], P('head'), may hold values from 0.25 to 1.75
- queries: bfloat16 [1536, 8192], P('seq', 'head'), may hold values from -48 to 48
- new_keys: bfloat16 [1536, 1024], P('seq'), may hold values from -6 to 6
- new_values: bfloat16 [1536, 1024], P('seq'), may hold values from -6 to 6
- cache_keys: bfloat16 [1024, 1024], P('seq'), may hold values from -127 to 127, as said below
- cache_values: bfloat16 [1024, 1024], P('seq'), may hold values from -127 to 127, as said below
- cache_key_scale: float32 [1024], replicated, may hold values from 0.003 to 0.03
- cache_value_scale: float32 [1024], replicated, may hold values from 0.003 to 0.03
Outputs:
- ssm_output: bfloat16 [1536, 16384], P('seq', 'head')
- attended: bfloat16 [1536, 8192], P('seq', 'head')
- key_codes: bfloat16 [1536, 1024], P('seq')
- key_scale: float32 [1024], replicated
Inputs may be any that keep to these rules, and one draw needn't show every extreme that they name: `cache_keys`: whole numbers. `cache_values`: whole numbers.
All inputs are finite; a program needn't handle non-finite values.
Results may differ from a plain program's by a relative error of at most 0.019.
Values may be sent and summed in bfloat16 or wider, within the bound.
A program may use at most 128 MiB of HBM per device.

v0:
```python
import functools
import jax
import jax.numpy as jnp
from jax import lax
from jax.experimental import pallas as pl
from jax.experimental.pallas import tpu as pltpu
from jax.sharding import PartitionSpec as P

SSM_HEADS = 256
HEAD_DIM = 64
STATE = 256
GROUPS = 8
ATT_HEADS = 64
KV_HEADS = 8
ATT_DIM = 128

NEG = -1e30
LOG2E = 1.4426950408889634
HIGHEST = lax.Precision.HIGHEST
MESH = pl.DeviceIdType.MESH
VMEM = pl.BlockSpec(memory_space=pltpu.VMEM)
F32 = jnp.float32
BF16 = jnp.bfloat16


def iota(shape, axis):
    return lax.broadcasted_iota(jnp.int32, shape, axis)


def lanes(start, size):
    return pl.ds(pl.multiple_of(start, 128), size)


def local_kernel(
    x_ref,
    sin_ref,
    sout_ref,
    step_ref,
    decay_ref,
    forget_ref,
    skip_ref,
    nk_ref,
    nv_ref,
    ck_ref,
    cv_ref,
    cks_ref,
    cvs_ref,
    state_ref,
    run_ref,
    fade_ref,
    at_ref,
    gram_ref,
    meta_ref,
    kvc_ref,
    kvn_ref,
):
    tokens, width = x_ref.shape
    heads = step_ref.shape[0]
    per_group = min(SSM_HEADS // GROUPS, heads)
    groups_here = heads // per_group
    z = lax.axis_index("head")
    group0 = z * heads // (SSM_HEADS // GROUPS)
    kvw = kvc_ref.shape[1] // 2
    q_heads = heads * ATT_HEADS // SSM_HEADS
    first = z * q_heads // (ATT_HEADS // KV_HEADS)
    cols = lanes(first * ATT_DIM, kvw)
    kvc_ref[:, :kvw] = (ck_ref[:, cols].astype(F32) * cks_ref[:, cols]).astype(BF16)
    kvc_ref[:, kvw:] = (cv_ref[:, cols].astype(F32) * cvs_ref[:, cols]).astype(BF16)
    kvn_ref[:, :kvw] = nk_ref[:, cols]
    kvn_ref[:, kvw:] = nv_ref[:, cols]
    meta_ref[:, width:] = jnp.max(jnp.abs(nk_ref[...].astype(F32)), axis=0, keepdims=True)

    row, col = iota((tokens, tokens), 0), iota((tokens, tokens), 1)
    lower = jnp.where(col <= row, 1.0, 0.0)
    eye = jnp.where(col == row, 1.0, 0.0)
    step = step_ref[...].T
    forgotten = jnp.sum(lower * forget_ref[...], axis=1, keepdims=True)
    decayed = jnp.dot(
        lower, decay_ref[...] * step, precision=HIGHEST, preferred_element_type=F32
    )
    running = -(decayed + forgotten) * LOG2E
    start = running - jnp.log2(step)
    at_ref[...] = start.T
    rest = jnp.concatenate(
        [running, jnp.broadcast_to(skip_ref[...], (16, heads))], axis=0
    )
    for third in range(3):
        piece = rest.astype(BF16)
        run_ref[:, third * heads : (third + 1) * heads] = piece
        rest = rest - piece.astype(F32)
    fade_ref[...] = jnp.exp2(running).astype(BF16)
    tail = jnp.exp2(running[tokens - 1 : tokens] - start).astype(BF16)
    last = running[tokens - 8 : tokens]
    block = min(512, width)
    for g in range(groups_here):
        gcols = lanes((group0 + g) * STATE, STATE)
        maps_in = sin_ref[:, gcols]
        gram_ref[g] = lax.dot_general(
            sout_ref[:, gcols], maps_in, (((1,), (1,)), ((), ())), preferred_element_type=F32
        )
        turned = lax.dot_general(
            maps_in,
            eye.astype(BF16),
            (((0,), (0,)), ((), ())),
            preferred_element_type=F32,
        ).astype(BF16)
        for b in range(per_group * HEAD_DIM // block):
            begin = g * per_group * HEAD_DIM + b * block
            here = pl.ds(begin, block)
            pick = choose(heads, begin, block)
            meta_ref[:, here] = jnp.dot(
                last, pick, precision=HIGHEST, preferred_element_type=F32
            )[7:8]
            scale = jnp.dot(tail, pick.astype(BF16), preferred_element_type=F32)
            scaled = (x_ref[:, here].astype(F32) * scale).astype(BF16)
            state_ref[:, here] = jnp.dot(
                turned, scaled, preferred_element_type=F32
            ).astype(BF16)


def choose(heads, begin, size):
    lane = begin + iota((heads, size), 1)
    return (iota((heads, size), 0) == lane // HEAD_DIM).astype(F32)


def within_pair(p, x_ref, run_ref, at_ref, gram_ref, part_ref):
    tokens = x_ref.shape[0]
    heads = run_ref.shape[1] // 3
    per_group = min(SSM_HEADS // GROUPS, heads)
    here = lanes(p * 128, 128)
    pick = choose(heads, p * 128, 128).astype(BF16)
    both = jnp.dot(
        run_ref[...], jnp.concatenate([pick] * 3, axis=0), preferred_element_type=F32
    )
    run, skip = both[:tokens], both[tokens : tokens + 1]
    x = x_ref[:, here]
    gram = gram_ref[(2 * p) // per_group]
    causal = iota((tokens, tokens), 1) <= iota((tokens, tokens), 0)

    def one(k):
        spread = run[:, k * HEAD_DIM : k * HEAD_DIM + 1] - at_ref[pl.ds(2 * p + k, 1), :]
        return (jnp.exp2(jnp.where(causal, spread, NEG)) * gram).astype(BF16)

    pair = jnp.dot(
        jnp.concatenate([one(0), one(1)], axis=0), x, preferred_element_type=F32
    )
    y = jnp.where(iota((tokens, 128), 1) < HEAD_DIM, pair[:tokens], pair[tokens:])
    part_ref[:, here] = (y + skip * x.astype(F32)).astype(BF16)


def attend(h, q_ref, allc_ref, alln_ref, bias_ref, vc_ref, vn_ref, att_ref):
    q_heads = q_ref.shape[1] // ATT_DIM
    kv_here = vc_ref.shape[0]
    share = q_heads // kv_here
    together = 2 if share % 2 == 0 else 1
    tokens = q_ref.shape[0]
    k = (h * together) // share
    factor = ATT_DIM**-0.5 * LOG2E
    nt = (((1,), (1,)), ((), ()))
    own = [lanes((h * together + e) * ATT_DIM, ATT_DIM) for e in range(together)]
    q = jnp.concatenate([q_ref[:, o] for o in own], axis=0)
    at = lanes(k * ATT_DIM, ATT_DIM)
    keys_c = allc_ref[:, :, at].reshape(-1, ATT_DIM)
    keys_n = alln_ref[:, :, at].reshape(-1, ATT_DIM)
    old = lax.dot_general(q, keys_c, nt, preferred_element_type=F32)
    new = lax.dot_general(q, keys_n, nt, preferred_element_type=F32)
    bias = bias_ref[...]
    new = (new.reshape(together, tokens, -1) + bias[None]).reshape(together * tokens, -1)
    peak = jnp.maximum(
        jnp.max(old, axis=1, keepdims=True), jnp.max(new, axis=1, keepdims=True)
    )
    old = jnp.exp2((old - peak) * factor).astype(BF16)
    new = jnp.exp2((new - peak) * factor).astype(BF16)
    both = jnp.dot(old, vc_ref[k], preferred_element_type=F32) + jnp.dot(
        new, vn_ref[k], preferred_element_type=F32
    )
    result = (both[:, :ATT_DIM] / both[:, ATT_DIM:]).astype(BF16)
    for e in range(together):
        att_ref[:, own[e]] = result[e * tokens : (e + 1) * tokens]


def comm_kernel(
    n,
    chunks,
    state_ref,
    kvc_ref,
    kvn_ref,
    meta_ref,
    x_ref,
    run_ref,
    at_ref,
    gram_ref,
    q_ref,
    out_ref,
    allm_ref,
    part_ref,
    att_ref,
    allc_ref,
    alln_ref,
    vc_ref,
    vn_ref,
    bias_ref,
    sib_ref,
    own_ref,
    incl_ref,
    recv_ref,
    back_ref,
    meta_s,
    meta_r,
    kv_s,
    kv_r,
    kv_f,
    sib_s,
    sib_r,
    pre_s,
    pre_r,
    rel_s,
    back_s,
    back_r,
):
    n2 = n // 2
    levels = n2.bit_length() - 1
    me = lax.axis_index("seq")
    i, c = me % 2, me // 2
    other = me + 1 - 2 * i
    width = state_ref.shape[1]
    half = width // 2
    size = half // chunks

    barrier = pltpu.get_barrier_semaphore()
    for d in range(1, n):
        pl.semaphore_signal(
            barrier, inc=1, device_id={"seq": (me + d) % n}, device_id_type=MESH
        )
    pl.semaphore_wait(barrier, n - 1)

    def remote(src, dst, ssem, rsem, to):
        return pltpu.make_async_remote_copy(
            src_ref=src,
            dst_ref=dst,
            send_sem=ssem,
            recv_sem=rsem,
            device_id={"seq": to},
            device_id_type=MESH,
        )

    def sib_copy(j):
        return remote(
            state_ref.at[:, lanes((1 - i) * half + j * size, size)],
            sib_ref.at[j],
            sib_s.at[j],
            sib_r.at[j],
            other,
        )

    for j in range(chunks):
        sib_copy(j).start()
    for d in range(1, n):
        remote(
            meta_ref, allm_ref.at[me], meta_s.at[d], meta_r.at[me], (me + d) % n
        ).start()

    def cache_copy(d, to):
        return remote(kvc_ref, allc_ref.at[me], kv_s.at[0, d], kv_r.at[0, me], to)

    def new_copy(d, to):
        return remote(kvn_ref, alln_ref.at[me], kv_s.at[1, d], kv_r.at[1, me], to)

    cache_copy(0, other).start()
    new_copy(0, other).start()
    for d in range(1, n2):
        to = ((c + d) % n2) * 2 + i
        cache_copy(d, to).start()

        @pl.when(c + d < n2)
        def _():
            new_copy(d, to).start()

    allm_ref[me] = meta_ref[...]
    allc_ref[me] = kvc_ref[...]
    alln_ref[me] = kvn_ref[...]
    for d in range(1, n2):
        later = c + d

        @pl.when(later < n2)
        def _():
            for k in range(2):
                alln_ref[later * 2 + k] = jnp.zeros(kvn_ref.shape, BF16)

    for d in range(1, n):
        r = (me + d) % n
        remote(meta_ref, allm_ref.at[r], meta_s.at[d], meta_r.at[r], r).wait_recv()

    def sends(l):
        return c % (2 ** (l + 1)) == 2**l - 1

    def targets(l):
        return [0] if l == 0 else list(range(1, 2**l, 2))

    def pre_copy(l, j, r):
        return remote(
            incl_ref.at[l, j],
            recv_ref.at[l, j],
            pre_s.at[l, j, r],
            pre_r.at[l, j],
            ((c + 1 + r) % n2) * 2 + i,
        )

    def relay_copy(l, j):
        return remote(
            recv_ref.at[l, j],
            recv_ref.at[l, j],
            rel_s.at[l, j],
            pre_r.at[l, j],
            ((c + n2 - 1) % n2) * 2 + i,
        )

    def logs(r, j):
        return allm_ref[r, :, lanes(i * half + j * size, size)]

    def gather_first(j, _):
        sib_copy(j).wait_recv()
        mine = state_ref[:, lanes(i * half + j * size, size)].astype(F32)
        theirs = sib_ref[j].astype(F32)
        d1 = jnp.exp2(logs(2 * c + 1, j))
        total = jnp.where(i == 0, d1 * mine + theirs, d1 * theirs + mine)
        incl_ref[0, j] = total.astype(BF16)
        own_ref[j] = jnp.zeros(own_ref.shape[1:], F32)

        @pl.when(sends(0))
        def _():
            pre_copy(0, j, 0).start()

        return 0

    lax.fori_loop(0, chunks, gather_first, 0)
    fresh = bias_ref.shape[1]
    tokens = x_ref.shape[0]
    seen = iota((tokens, fresh), 1) <= me * tokens + iota((tokens, fresh), 0)
    bias_ref[...] = jnp.where(seen, 0.0, NEG)
    pairs = width // 128
    early = n2
    ahead = pairs * 3 // 4

    def pair(p, _):
        within_pair(p, x_ref, run_ref, at_ref, gram_ref, part_ref)
        return 0


    def forward(kind, d):
        src = allc_ref if kind == 0 else alln_ref
        slot = ((c + d) % n2) * 2 + i
        return remote(
            src.at[slot], src.at[slot], kv_f.at[kind, d], kv_r.at[kind, slot], other
        )

    def combine(j, _):
        for l in range(levels):

            @pl.when(c % (2 ** (l + 1)) >= 2**l)
            def _():
                pre_copy(l, j, 0).wait_recv()
                if l >= 1:

                    @pl.when(c % 2 == 1)
                    def _():
                        relay_copy(l, j).start()

                base = c - c % (2**l)
                logsum = jnp.zeros((1, size), F32)
                for back in range(1, 2**l):
                    at = (c + n2 - back) % n2
                    both = logs(2 * at, j) + logs(2 * at + 1, j)
                    logsum += jnp.where(c - back >= base, both, 0.0)
                own_ref[j] = jnp.exp2(logsum) * recv_ref[l, j].astype(F32) + own_ref[j]

            if l + 1 < levels:

                @pl.when(sends(l + 1))
                def _():
                    keep = jnp.exp2(logs(2 * c, j) + logs(2 * c + 1, j))
                    incl_ref[l + 1, j] = (
                        keep * own_ref[j] + incl_ref[0, j].astype(F32)
                    ).astype(BF16)
                    for r in targets(l + 1):
                        pre_copy(l + 1, j, r).start()

        enter = own_ref[j]
        mine = state_ref[:, lanes(i * half + j * size, size)].astype(F32)
        first = jnp.where(i == 0, mine, sib_ref[j].astype(F32))
        middle = jnp.exp2(logs(2 * c, j)) * enter + first
        out_ref[:, lanes(i * half + j * size, size)] = jnp.where(
            i == 0, enter, middle
        ).astype(BF16)
        back_ref[j] = jnp.where(i == 0, middle, enter).astype(BF16)
        back_copy(j, i).start()
        return 0

    def remote_slot(kind, d):
        src = allc_ref if kind == 0 else alln_ref
        mine = kvc_ref if kind == 0 else kvn_ref
        slot = ((c + d) % n2) * 2 + i
        return remote(mine, src.at[slot], kv_s.at[kind, d], kv_r.at[kind, slot], slot)

    def back_copy(j, who):
        return remote(
            back_ref.at[j],
            out_ref.at[:, lanes(who * half + j * size, size)],
            back_s.at[j],
            back_r.at[j],
            other,
        )

    def first_part(j, _):
        lax.fori_loop(j * ahead // early, (j + 1) * ahead // early, pair, 0)
        for d in range(1, n2):

            @pl.when(j == d)
            def _():
                remote_slot(0, d).wait_recv()
                forward(0, d).start()

                @pl.when((c + d) % n2 < c)
                def _():
                    remote_slot(1, d).wait_recv()
                    forward(1, d).start()

        return 0

    lax.fori_loop(0, early, first_part, 0)

    def other_slot(kind, d):
        src = allc_ref if kind == 0 else alln_ref
        mine = kvc_ref if kind == 0 else kvn_ref
        slot = ((c + d) % n2) * 2 + (1 - i)
        return remote(mine, src.at[slot], kv_f.at[kind, d], kv_r.at[kind, slot], other)

    for d in range(n2):
        other_slot(0, d).wait_recv()
    other_slot(1, 0).wait_recv()
    for d in range(1, n2):

        @pl.when((c + d) % n2 < c)
        def _():
            other_slot(1, d).wait_recv()

    kv_here = vc_ref.shape[0]
    for k in range(kv_here):
        at = (kv_here + k) * ATT_DIM
        for all_ref, ext_ref in ((allc_ref, vc_ref), (alln_ref, vn_ref)):
            ext_ref[k, :, :ATT_DIM] = all_ref[:, :, at : at + ATT_DIM].reshape(-1, ATT_DIM)
            ext_ref[k, :, ATT_DIM:] = jnp.ones((ext_ref.shape[1], ATT_DIM), BF16)

    q_heads = q_ref.shape[1] // ATT_DIM
    steps = q_heads // 2 if (q_heads // kv_here) % 2 == 0 else q_heads

    def head(h, _):
        attend(h, q_ref, allc_ref, alln_ref, bias_ref, vc_ref, vn_ref, att_ref)
        return 0

    def second_part(j, _):
        rest = pairs - ahead
        lax.fori_loop(
            ahead + j * rest // chunks, ahead + (j + 1) * rest // chunks, pair, 0
        )
        lax.fori_loop(j * steps // chunks, (j + 1) * steps // chunks, head, 0)
        combine(j, 0)
        return 0

    lax.fori_loop(0, chunks, second_part, 0)

    def drain(j, _):
        back_copy(j, 1 - i).wait_recv()
        back_copy(j, i).wait_send()
        sib_copy(j).wait_send()
        for l in range(levels):

            @pl.when(sends(l))
            def _():
                for r in targets(l):
                    pre_copy(l, j, r).wait_send()

            if l >= 1:

                @pl.when((c % (2 ** (l + 1)) >= 2**l) & (c % 2 == 1))
                def _():
                    relay_copy(l, j).wait_send()

        return 0

    lax.fori_loop(0, chunks, drain, 0)
    for d in range(1, n):
        remote(
            meta_ref, allm_ref.at[me], meta_s.at[d], meta_r.at[me], (me + d) % n
        ).wait_send()
    cache_copy(0, other).wait_send()
    new_copy(0, other).wait_send()
    for d in range(1, n2):
        to = ((c + d) % n2) * 2 + i
        cache_copy(d, to).wait_send()
        forward(0, d).wait_send()

        @pl.when(c + d < n2)
        def _():
            new_copy(d, to).wait_send()

        @pl.when((c + d) % n2 < c)
        def _():
            forward(1, d).wait_send()


def final_kernel(
    part_ref,
    fade_ref,
    sout_ref,
    state_ref,
    meta_ref,
    nk_ref,
    y_ref,
    code_ref,
    scale_ref,
):
    tokens, width = part_ref.shape
    heads = fade_ref.shape[1]
    per_group = min(SSM_HEADS // GROUPS, heads)
    z = lax.axis_index("head")
    group0 = z * heads // (SSM_HEADS // GROUPS)
    block = min(512, width)

    magnitude = jnp.max(meta_ref[:, 0, width:], axis=0, keepdims=True)
    scale = (magnitude + 1e-6) / 127.0
    scale_ref[...] = scale
    code_ref[...] = (nk_ref[...].astype(F32) / scale).astype(BF16)
    fade = fade_ref[...]
    for b in range(width // block):
        here = pl.ds(b * block, block)
        g = group0 + (b * block) // (per_group * HEAD_DIM)
        prior = jnp.dot(
            sout_ref[:, lanes(g * STATE, STATE)], state_ref[:, here], preferred_element_type=F32
        )
        pick = choose(heads, b * block, block).astype(BF16)
        spread = jnp.dot(fade, pick, preferred_element_type=F32)
        y_ref[:, here] = (part_ref[:, here].astype(F32) + spread * prior).astype(BF16)


def body(
    n,
    ssm_input,
    state_in,
    state_out,
    step_size,
    decay_rate,
    forget,
    skip_gain,
    queries,
    new_keys,
    new_values,
    cache_keys,
    cache_values,
    cache_key_scale,
    cache_value_scale,
):
    tokens, width = ssm_input.shape
    heads = step_size.shape[1]
    rows = cache_keys.shape[0]
    channels = new_keys.shape[1]
    q_heads = queries.shape[1] // ATT_DIM
    kv_here = max(1, q_heads // (ATT_HEADS // KV_HEADS))
    kvw = kv_here * ATT_DIM
    per_group = min(SSM_HEADS // GROUPS, heads)
    groups_here = heads // per_group
    limit = pltpu.CompilerParams(vmem_limit_bytes=60 * 1024 * 1024)
    shape = jax.ShapeDtypeStruct
    state, run, fade, at, gram, meta, kvc, kvn = pl.pallas_call(
        local_kernel,
        out_shape=(
            shape((STATE, width), BF16),
            shape((tokens + 16, 3 * heads), BF16),
            shape((tokens, heads), BF16),
            shape((heads, tokens), F32),
            shape((groups_here, tokens, tokens), F32),
            shape((1, width + channels), F32),
            shape((rows, 2 * kvw), BF16),
            shape((tokens, 2 * kvw), BF16),
        ),
        in_specs=[VMEM] * 13,
        out_specs=(VMEM,) * 8,
        compiler_params=limit,
        name="local",
    )(
        ssm_input,
        state_in,
        state_out,
        step_size.T,
        decay_rate.reshape(1, heads),
        forget.reshape(1, tokens),
        skip_gain.reshape(1, heads),
        new_keys,
        new_values,
        cache_keys,
        cache_values,
        cache_key_scale.reshape(1, channels),
        cache_value_scale.reshape(1, channels),
    )
    half = width // 2
    size = min(256, half)
    chunks = half // size
    n2 = n // 2
    levels = n2.bit_length() - 1
    fan = max(1, n2 // 2)
    dma = pltpu.SemaphoreType.DMA
    carried, allm, part, attended = pl.pallas_call(
        functools.partial(comm_kernel, n, chunks),
        out_shape=(
            shape((STATE, width), BF16),
            shape((n, 1, width + channels), F32),
            shape((tokens, width), BF16),
            shape((tokens, queries.shape[1]), BF16),
        ),
        in_specs=[VMEM] * 9,
        out_specs=(VMEM,) * 4,
        scratch_shapes=[
            pltpu.VMEM((n, rows, 2 * kvw), BF16),
            pltpu.VMEM((n, tokens, 2 * kvw), BF16),
            pltpu.VMEM((kv_here, n * rows, 2 * ATT_DIM), BF16),
            pltpu.VMEM((kv_here, n * tokens, 2 * ATT_DIM), BF16),
            pltpu.VMEM((tokens, n * tokens), F32),
            pltpu.VMEM((chunks, STATE, size), BF16),
            pltpu.VMEM((chunks, STATE, size), F32),
            pltpu.VMEM((levels, chunks, STATE, size), BF16),
            pltpu.VMEM((levels, chunks, STATE, size), BF16),
            pltpu.VMEM((chunks, STATE, size), BF16),
            dma((n,)),
            dma((n,)),
            dma((2, n2)),
            dma((2, n)),
            dma((2, n2)),
            dma((chunks,)),
            dma((chunks,)),
            dma((levels, chunks, fan)),
            dma((levels, chunks)),
            dma((levels, chunks)),
            dma((chunks,)),
            dma((chunks,)),
        ],
        compiler_params=pltpu.CompilerParams(
            collective_id=0, has_side_effects=True, vmem_limit_bytes=60 * 1024 * 1024
        ),
        name="exchange",
    )(state, kvc, kvn, meta, ssm_input, run, at, gram, queries)
    y, codes, scale = pl.pallas_call(
        final_kernel,
        out_shape=(
            shape((tokens, width), BF16),
            shape((tokens, channels), BF16),
            shape((1, channels), F32),
        ),
        in_specs=[VMEM] * 6,
        out_specs=(VMEM,) * 3,
        compiler_params=limit,
        name="finish",
    )(part, fade, state_out, carried, allm, new_keys)
    return (y, attended, codes, scale.reshape(channels))


def solution(mesh):
    in_specs = (
        P("seq", "head"),
        P("seq", None),
        P("seq", None),
        P("seq", "head"),
        P("head"),
        P("seq"),
        P("head"),
        P("seq", "head"),
        P("seq", None),
        P("seq", None),
        P("seq", None),
        P("seq", None),
        P(),
        P(),
    )
    out_specs = (P("seq", "head"), P("seq", "head"), P("seq", None), P())
    return jax.shard_map(
        functools.partial(body, mesh.shape["seq"]),
        mesh=mesh,
        in_specs=in_specs,
        out_specs=out_specs,
        check_vma=False,
    )
```

profile of v0, /device:TPU:29, one launch (start us, length us, event | category | flops | bytes accessed | tf_op | source)
XLA Modules:
  0.0 76.6 jit_solution(2838290630261049441)
XLA Ops:
  0.6 6.8 %local.1 = (bf16[256,4096]{1,0:T(8,128)(2,1)}, bf16[208,192]{1,0:T(8,128)(2,1)}, bf16[192,64]{1,0:T(8,128)(2,1)}, f32[64,192]{1,0:T(8,128)}, f32[2,192,192]{2,1,...) custom-call(bf16[192,4096]{1,0:T(8,128)(2,1)} %x_ref.3, ...), custom_call_target="tpu_custom_call" | custom-call | tf_op jit(solution)/shard_map/local/pallas_call | solution.py:574
  7.4 63.5 %exchange.1 = (bf16[256,4096]{1,0:T(8,128)(2,1)}, f32[8,1,5120]{2,1,0:T(1,128)}, bf16[192,4096]{1,0:T(8,128)(2,1)}, bf16[192,2048]{1,0:T(8,128)(2,1)}) custom-call(bf16[256,4096]{1,0:T(8,128)(2,1)} %get-tuple-element.19.state_ref, bf16[128,512]{1,0:T(8,128)(2,1)} %get-tuple-element.20.kvc_ref, bf16[192,512]{1,0:T(8,128)(2,1)} %get-tuple-element.21.kvn_ref, ...), custom_call_target="tpu_custom_call" | custom-call | tf_op jit(solution)/shard_map/exchange/pallas_call | solution.py:612
  70.9 0.0 copy-start
  70.9 4.8 %finish.1 = (bf16[192,4096]{1,0:T(8,128)(2,1)}, bf16[192,1024]{1,0:T(8,128)(2,1)}, f32[1,1024]{1,0:T(1,128)}) custom-call(bf16[192,4096]{1,0:T(8,128)(2,1)} %get-tuple-element.26.part_ref, bf16[192,64]{1,0:T(8,128)(2,1)} %get-tuple-element.27.fade_ref, bf16[192,2048]{1,0:T(8,128)(2,1)} %sout_ref.3, bf16[256,4096]{1,0:T(8,128)(2,1)} %get-tuple-element.28.state_ref, ...), custom_call_target="tpu_custom_call" | custom-call | tf_op jit(solution)/shard_map/finish/pallas_call | solution.py:651
  75.7 0.0 copy-done
  75.7 0.9 %copy.19 = bf16[192,2048]{1,0:T(8,128)(2,1)} copy(bf16[192,2048]{1,0:T(8,128)(2,1)S(1)} %copy-done) | data formatting | bytes 1572864
Async XLA Ops:
  70.9 4.8 %copy-start = (bf16[192,2048]{1,0:T(8,128)(2,1)S(1)}, bf16[192,2048]{1,0:T(8,128)(2,1)}, u32[]{:S(2)}) copy-start(bf16[192,2048]{1,0:T(8,128)(2,1)} %get-tuple-element.39) | copy-start | bytes 2359300
where the time goes:
time: 76.8 us; the launch traced here: 76.6 us
  Pallas kernels  75.1 us (98%)
  local copies, waits for them, and re-layouts  0.88 us (1%)
    pallas_call x1, Pallas kernels, body(): pl.pallas_call(functools.partial(comm_kernel, n, chunks), out_shape=(shap...  63.5 us
    pallas_call x1, Pallas kernels, body(): pl.pallas_call(local_kernel, out_shape=(shape((STATE, width), BF16), shap...  6.76 us
    pallas_call x1, Pallas kernels, body(): pl.pallas_call(final_kernel, out_shape=(shape((tokens, width), BF16), sha...  4.8 us

commit v1 on v0

--- a/solution.py
+++ b/solution.py
@@ -662,6 +662,773 @@
     )(part, fade, state_out, carried, allm, new_keys)
     return (y, attended, codes, scale.reshape(channels))
 
+BLOCK = 96
+
+
+def span_blocks(tokens):
+    return max(1, tokens // BLOCK)
+
+
+def split2(value):
+    high = value.astype(BF16)
+    low = (value - high.astype(F32)).astype(BF16)
+    return jnp.concatenate([high, low], axis=1)
+
+
+def choose2(heads, begin, size):
+    lane = begin + iota((2 * heads, size), 1)
+    row = iota((2 * heads, size), 0)
+    return (row % heads == lane // HEAD_DIM).astype(BF16)
+
+
+def factor_rows(tokens):
+    nb = span_blocks(tokens)
+    size = tokens // nb
+    places, at = {}, 0
+    for name, rows in (
+        [("z", tokens), ("tail", 16)]
+        + [(f"z{b}", (b + 1) * size) for b in range(nb - 1)]
+        + [("out", tokens), ("skip", 16), ("fade", tokens)]
+    ):
+        places[name] = (at, at + rows)
+        at += rows
+    return places, at
+
+
+def with_ones(v):
+    return jnp.concatenate([v, jnp.ones(v.shape, BF16)], axis=1)
+
+
+def attend_visible(step, streams, together, chip, q_ref, allc_ref, alln_ref, bias_ref, att_ref):
+    tokens = q_ref.shape[0]
+    kvw = allc_ref.shape[2] // 2
+    share = (q_ref.shape[1] // ATT_DIM) // (kvw // ATT_DIM)
+    factor = ATT_DIM**-0.5 * LOG2E
+    nt = (((1,), (1,)), ((), ()))
+    k = (step * streams * together) // share
+    at, av = lanes(k * ATT_DIM, ATT_DIM), lanes(kvw + k * ATT_DIM, ATT_DIM)
+    seen = 2 * chip + 2
+
+    def rows_of(cols):
+        return jnp.concatenate(
+            [
+                allc_ref[:, :, cols].reshape(-1, ATT_DIM),
+                alln_ref[:seen, :, cols].reshape(-1, ATT_DIM),
+            ],
+            axis=0,
+        )
+
+    keys, values = rows_of(at), with_ones(rows_of(av))
+    free = keys.shape[0] - 2 * tokens
+    own, scores = [], []
+    for e in range(streams):
+        first = (step * streams + e) * together
+        own.append([lanes((first + f) * ATT_DIM, ATT_DIM) for f in range(together)])
+        q = jnp.concatenate([q_ref[:, o] for o in own[e]], axis=0)
+        scores.append(lax.dot_general(q, keys, nt, preferred_element_type=F32))
+    bias = bias_ref[...]
+    for e in range(streams):
+        near = scores[e][:, free:].reshape(together, tokens, -1) + bias[None]
+        s = jnp.concatenate([scores[e][:, :free], near.reshape(together * tokens, -1)], axis=1)
+        peak = jnp.max(s, axis=1, keepdims=True)
+        p = jnp.exp2((s - peak) * factor).astype(BF16)
+        both = jnp.dot(p, values, preferred_element_type=F32)
+        result = (both[:, :ATT_DIM] / both[:, ATT_DIM:]).astype(BF16)
+        for f, o in enumerate(own[e]):
+            att_ref[:, o] = result[f * tokens : (f + 1) * tokens]
+
+
+def fused_kernel(
+    chunks,
+    x_hbm,
+    sin_hbm,
+    sout_hbm,
+    step_ref,
+    decay_ref,
+    forget_ref,
+    skip_ref,
+    q_hbm,
+    nk_hbm,
+    nv_hbm,
+    ck_hbm,
+    cv_hbm,
+    cks_ref,
+    cvs_ref,
+    y_ref,
+    att_ref,
+    mag_ref,
+    x_ref,
+    sin_ref,
+    sout_ref,
+    q_ref,
+    nk_ref,
+    nv_ref,
+    ck_ref,
+    cv_ref,
+    kvc_ref,
+    kvn_ref,
+    allc_ref,
+    alln_ref,
+    bias_ref,
+    meta_ref,
+    allm_ref,
+    fac_ref,
+    fade_ref,
+    z_ref,
+    gram_ref,
+    turned_ref,
+    give_ref,
+    sib_ref,
+    mine_ref,
+    full_ref,
+    tx_ref,
+    rx_ref,
+    enter_ref,
+    back_ref,
+    other_ref,
+    load_s,
+    meta_s,
+    meta_r,
+    kv_s,
+    kv_r,
+    kv_f,
+    kv_p,
+    sib_s,
+    sib_r,
+    out_s,
+    in_r,
+    back_s,
+    back_r,
+):
+    n = 8
+    tokens, width = x_ref.shape
+    heads = step_ref.shape[0]
+    per_group = min(SSM_HEADS // GROUPS, heads)
+    groups_here = heads // per_group
+    channels = nk_ref.shape[1]
+    kvw = kvc_ref.shape[1] // 2
+    half = width // 2
+    size = half // chunks
+    near = chunks // 2
+    places, _ = factor_rows(tokens)
+    nb = span_blocks(tokens)
+    bs = tokens // nb
+
+    me = lax.axis_index("seq")
+    z = lax.axis_index("head")
+    i, c = me % 2, me // 2
+    other = me + 1 - 2 * i
+    cx, cy = c + 1 - 2 * (c % 2), (c + 2) % 4
+    cd = 3 - c
+    group0 = z * heads // (SSM_HEADS // GROUPS)
+    q_heads = heads * ATT_HEADS // SSM_HEADS
+    first_kv = z * q_heads // (ATT_HEADS // KV_HEADS)
+    cols = lanes(first_kv * ATT_DIM, kvw)
+    gcols = lanes(group0 * STATE, groups_here * STATE)
+
+    barrier = pltpu.get_barrier_semaphore()
+    for d in range(1, n):
+        pl.semaphore_signal(
+            barrier, inc=1, device_id={"seq": (me + d) % n}, device_id_type=MESH
+        )
+
+    loads = [
+        pltpu.make_async_copy(src, dst, load_s.at[k])
+        for k, (src, dst) in enumerate(
+            [
+                (ck_hbm.at[:, cols], ck_ref),
+                (cv_hbm.at[:, cols], cv_ref),
+                (nk_hbm, nk_ref),
+                (nv_hbm.at[:, cols], nv_ref),
+                (sin_hbm.at[:, gcols], sin_ref),
+                (sout_hbm.at[:, gcols], sout_ref),
+                (x_hbm, x_ref),
+                (q_hbm, q_ref),
+            ]
+        )
+    ]
+    for copy in loads:
+        copy.start()
+
+    def remote(src, dst, ssem, rsem, to):
+        return pltpu.make_async_remote_copy(
+            src_ref=src,
+            dst_ref=dst,
+            send_sem=ssem,
+            recv_sem=rsem,
+            device_id={"seq": to},
+            device_id_type=MESH,
+        )
+
+    def dev(chip):
+        return chip * 2 + i
+
+    alls = (allc_ref, alln_ref)
+    owns = (kvc_ref, kvn_ref)
+
+    def own_copy(kind, way):
+        to = (other, dev(cx), dev(cy))[way]
+        return remote(
+            owns[kind], alls[kind].at[me], kv_s.at[kind, way], kv_r.at[kind, me], to
+        )
+
+    def pass_copy(kind, way, chip, to):
+        slot = dev(chip)
+        return remote(
+            alls[kind].at[slot],
+            alls[kind].at[slot],
+            kv_p.at[kind, way],
+            kv_r.at[kind, slot],
+            dev(to),
+        )
+
+    def forward(kind, chip):
+        slot = dev(chip)
+        return remote(
+            alls[kind].at[slot],
+            alls[kind].at[slot],
+            kv_f.at[kind, chip],
+            kv_r.at[kind, slot],
+            other,
+        )
+
+    def arrived(kind, slot):
+        remote(
+            owns[kind], alls[kind].at[slot], kv_s.at[kind, 0], kv_r.at[kind, slot], other
+        ).wait_recv()
+
+    loads[0].wait()
+    loads[1].wait()
+    kvc_ref[:, :kvw] = (ck_ref[...].astype(F32) * cks_ref[:, cols]).astype(BF16)
+    kvc_ref[:, kvw:] = (cv_ref[...].astype(F32) * cvs_ref[:, cols]).astype(BF16)
+    pl.semaphore_wait(barrier, n - 1)
+    for way in (1, 2, 0):
+        own_copy(0, way).start()
+    loads[2].wait()
+    loads[3].wait()
+    kvn_ref[:, :kvw] = nk_ref[:, cols]
+    kvn_ref[:, kvw:] = nv_ref[...]
+
+    @pl.when(cx > c)
+    def _():
+        own_copy(1, 1).start()
+
+    @pl.when(cy > c)
+    def _():
+        own_copy(1, 2).start()
+
+    own_copy(1, 0).start()
+
+    row, col = iota((tokens, tokens), 0), iota((tokens, tokens), 1)
+    lower = jnp.where(col <= row, 1.0, 0.0)
+    eye = jnp.where(col == row, 1.0, 0.0).astype(BF16)
+    step = step_ref[...].T
+    forgotten = jnp.sum(lower * forget_ref[...], axis=1, keepdims=True)
+    decayed = jnp.dot(
+        lower, decay_ref[...] * step, precision=HIGHEST, preferred_element_type=F32
+    )
+    running = -(decayed + forgotten) * LOG2E
+    start = running - jnp.log2(step)
+    last = running[tokens - 1 : tokens]
+    middles = [running[b * bs + bs // 2 - 1 : b * bs + bs // 2] for b in range(nb)]
+
+    meta_ref[:, :channels] = jnp.max(jnp.abs(nk_ref[...].astype(F32)), axis=0, keepdims=True)
+    meta_ref[:, channels:] = jnp.concatenate([last, jnp.zeros((1, 128 - heads), F32)], axis=1)
+
+    def meta_copy(d):
+        return remote(
+            meta_ref, allm_ref.at[me], meta_s.at[d], meta_r.at[me], (me + d) % n
+        )
+
+    def meta_arrived(r):
+        remote(meta_ref, allm_ref.at[r], meta_s.at[1], meta_r.at[r], r).wait_recv()
+
+    for d in range(1, n):
+        meta_copy(d).start()
+    allm_ref[me] = meta_ref[...]
+
+    def put(name, value):
+        begin, end = places[name]
+        fac_ref[begin:end] = split2(jnp.broadcast_to(value, (end - begin, heads)))
+
+    put("z", jnp.exp2(middles[nb - 1] - start))
+    put("tail", jnp.exp2(last - middles[nb - 1]))
+    for b in range(nb - 1):
+        put(f"z{b}", jnp.exp2(middles[b] - start[: (b + 1) * bs]))
+    put(
+        "out",
+        jnp.concatenate(
+            [jnp.exp2(running[b * bs : (b + 1) * bs] - middles[b]) for b in range(nb)], axis=0
+        ),
+    )
+    put("skip", skip_ref[...])
+    put("fade", jnp.exp2(running))
+    loads[4].wait()
+    loads[5].wait()
+    for g in range(groups_here):
+        gc = slice(g * STATE, (g + 1) * STATE)
+        maps_in = sin_ref[:, gc]
+        gram = lax.dot_general(
+            sout_ref[:, gc], maps_in, (((1,), (1,)), ((), ())), preferred_element_type=F32
+        )
+        gram_ref[g] = jnp.where(col <= row, gram, 0.0).astype(BF16)
+        turned_ref[g] = lax.dot_general(
+            maps_in, eye, (((0,), (0,)), ((), ())), preferred_element_type=F32
+        ).astype(BF16)
+    loads[6].wait()
+
+    def spread(first, final, begin):
+        rows = fac_ref[places[first][0] : places[final][1]]
+        return jnp.dot(rows, choose2(heads, begin, size), preferred_element_type=F32)
+
+    def local_state(begin):
+        here = lanes(begin, size)
+        by = spread("z", "tail", begin)
+        scaled = (x_ref[:, here].astype(F32) * by[:tokens]).astype(BF16)
+        z_ref[:, here] = scaled
+        sums = jnp.dot(
+            turned_ref[begin // (per_group * HEAD_DIM)], scaled, preferred_element_type=F32
+        )
+        return (sums * by[tokens : tokens + 1]).astype(BF16)
+
+    def sib_copy(j):
+        return remote(give_ref.at[j], sib_ref.at[j], sib_s.at[j], sib_r.at[j], other)
+
+    shift = (c % 2) * (1 - c // 2) * near
+
+    def give(s, _):
+        j = (s + shift) % chunks
+        give_ref[j] = local_state((1 - i) * half + j * size)
+        sib_copy(j).start()
+        return 0
+
+    lax.fori_loop(0, chunks, give, 0)
+    meta_arrived(other)
+
+    def logs_of(r):
+        return allm_ref[r, :, channels : channels + heads]
+
+    def set_fades(third):
+        logs = jnp.concatenate(
+            [logs_of(2 * c), logs_of(2 * c + 1), third, jnp.zeros((13, heads), F32)], axis=0
+        )
+        fade_ref[...] = split2(jnp.exp2(logs))
+
+    def fades(j):
+        return jnp.dot(
+            fade_ref[...], choose2(heads, i * half + j * size, size), preferred_element_type=F32
+        )
+
+    set_fades(jnp.zeros((1, heads), F32))
+
+    def full_copy(j):
+        slot = jnp.where(c == 0, 0, 1)
+        return remote(
+            full_ref.at[j], rx_ref.at[slot, j], out_s.at[0, j], in_r.at[slot, j], dev(cx)
+        )
+
+    def full_sent(j):
+        return (c == 0) | ((c == 1) & (j >= near)) | ((c == 2) & (j < near))
+
+    def own(s, _):
+        j = (s + shift) % chunks
+        mine = local_state(i * half + j * size)
+        mine_ref[j] = mine
+        sib_copy(j).wait_recv()
+        mine, theirs = mine.astype(F32), sib_ref[j].astype(F32)
+        d1 = fades(j)[1:2]
+        full_ref[j] = jnp.where(i == 0, d1 * mine + theirs, d1 * theirs + mine).astype(BF16)
+
+        @pl.when(full_sent(j))
+        def _():
+            full_copy(j).start()
+
+        return 0
+
+    lax.fori_loop(0, chunks, own, 0)
+
+    def pass_cache():
+        arrived(0, dev(cx))
+
+        @pl.when(c >= 1)
+        def _():
+            pass_copy(0, 0, cx, cy).start()
+
+        forward(0, cx).start()
+        arrived(0, dev(cy))
+
+        @pl.when(c == 3)
+        def _():
+            pass_copy(0, 1, cy, cx).start()
+
+        forward(0, cy).start()
+
+    pass_cache()
+    bias_ref[...] = jnp.where(
+        iota((tokens, 2 * tokens), 1) <= i * tokens + iota((tokens, 2 * tokens), 0), 0.0, NEG
+    )
+
+    def within(s, _):
+        begin = s * size
+        here = lanes(begin, size)
+        by = spread("z0" if nb > 1 else "out", "skip", begin)
+        at = 0
+        gram = gram_ref[begin // (per_group * HEAD_DIM)]
+        x = x_ref[:, here].astype(F32)
+        parts = []
+        for b in range(nb):
+            high = (b + 1) * bs
+            if b + 1 < nb:
+                scaled = (x[:high] * by[at : at + high]).astype(BF16)
+                at += high
+            else:
+                scaled = z_ref[:, here]
+            parts.append(
+                jnp.dot(gram[b * bs : high, :high], scaled, preferred_element_type=F32)
+            )
+        y = by[at : at + tokens] * jnp.concatenate(parts, axis=0)
+        y_ref[:, here] = (y + by[at + tokens : at + tokens + 1] * x).astype(BF16)
+        return 0
+
+    lax.fori_loop(0, 2 * chunks, within, 0)
+
+    arrived(0, dev(cd))
+    forward(0, cd).start()
+
+    @pl.when(cx < c)
+    def _():
+        arrived(1, dev(cx))
+
+        @pl.when(c == 1)
+        def _():
+            pass_copy(1, 0, cx, cy).start()
+
+        forward(1, cx).start()
+
+    @pl.when(cy < c)
+    def _():
+        arrived(1, dev(cy))
+
+        @pl.when(c == 3)
+        def _():
+            pass_copy(1, 1, cy, cx).start()
+
+        forward(1, cy).start()
+
+    for d in range(1, n):
+        r = (me + d) % n
+
+        @pl.when(r != other)
+        def _():
+            meta_arrived(r)
+
+    chip = jnp.where(c == 0, 1, jnp.where(c == 3, 2, c))
+    set_fades(logs_of(2 * chip) + logs_of(2 * chip + 1))
+    mag_ref[...] = jnp.max(allm_ref[:, 0, :channels], axis=0, keepdims=True)
+
+    @pl.when(cd < c)
+    def _():
+        arrived(1, dev(cd))
+        forward(1, cd).start()
+
+    allc_ref[me] = kvc_ref[...]
+    alln_ref[me] = kvn_ref[...]
+    arrived(0, other)
+    arrived(1, other)
+    for d in range(1, 4):
+        there = (c + d) % 4
+        arrived(0, there * 2 + 1 - i)
+
+        @pl.when(there < c)
+        def _():
+            arrived(1, there * 2 + 1 - i)
+
+    loads[7].wait()
+
+    def order(s):
+        left = (1 - c // 2) * ((s + near) % chunks) + (c // 2) * (near * (1 - s % 2) + s // 2)
+        return (c % 2) * s + (1 - c % 2) * left
+
+    def prior(begin, carried):
+        here = lanes(begin, size)
+        group = begin // (per_group * HEAD_DIM)
+        term = jnp.dot(sout_ref[:, lanes(group * STATE, STATE)], carried, preferred_element_type=F32)
+        by = spread("fade", "fade", begin)
+        y_ref[:, here] = (y_ref[:, here].astype(F32) + by * term).astype(BF16)
+
+    def rx_wait(slot, j):
+        remote(
+            full_ref.at[j], rx_ref.at[slot, j], out_s.at[0, j], in_r.at[slot, j], dev(cx)
+        ).wait_recv()
+
+    def tx_copy(j, chip):
+        return remote(tx_ref.at[j], rx_ref.at[0, j], out_s.at[1, j], in_r.at[0, j], dev(chip))
+
+    def relay_copy(j):
+        return remote(
+            rx_ref.at[0, j], rx_ref.at[0, j], out_s.at[2, j], in_r.at[0, j], dev(cx)
+        )
+
+    def back_copy(j):
+        return remote(back_ref.at[j], other_ref.at[j], back_s.at[j], back_r.at[j], other)
+
+    def combine(s):
+        j = order(s)
+        by = fades(j)
+        d0, keep = by[0:1], by[2:3]
+
+        @pl.when(c > 0)
+        def _():
+            rx_wait(0, j)
+
+        @pl.when((c == 3) & (j < near))
+        def _():
+            relay_copy(j).start()
+            rx_wait(1, j)
+            enter_ref[...] = keep * rx_ref[0, j].astype(F32) + rx_ref[1, j].astype(F32)
+
+        @pl.when(((c == 1) & (j < near)) | ((c == 2) & (j >= near)))
+        def _():
+            tx_ref[j] = (keep * rx_ref[0, j].astype(F32) + full_ref[j].astype(F32)).astype(BF16)
+            tx_copy(j, 3).start()
+
+        @pl.when((c == 0) & (j >= near))
+        def _():
+            rx_wait(1, j)
+            tx_ref[j] = (keep * full_ref[j].astype(F32) + rx_ref[1, j].astype(F32)).astype(BF16)
+            tx_copy(j, 2).start()
+
+        @pl.when(c == 0)
+        def _():
+            enter_ref[...] = jnp.zeros(enter_ref.shape, F32)
+
+        @pl.when((c == 1) | (c == 2) | ((c == 3) & (j >= near)))
+        def _():
+            enter_ref[...] = rx_ref[0, j].astype(F32)
+
+        enter = enter_ref[...]
+        first = jnp.where(i == 0, mine_ref[j].astype(F32), sib_ref[j].astype(F32))
+        middle = d0 * enter + first
+        back_ref[j] = jnp.where(i == 0, middle, enter).astype(BF16)
+        back_copy(j).start()
+        prior(i * half + j * size, jnp.where(i == 0, enter, middle).astype(BF16))
+
+    def returned(s):
+        j = order(s)
+        back_copy(j).wait_recv()
+        prior((1 - i) * half + j * size, other_ref[j])
+
+    def slot(s, _):
+        combine(s)
+
+        @pl.when(s > 0)
+        def _():
+            returned(s - 1)
+
+        return 0
+
+    streams, together = 2, 2
+    steps = q_heads // (streams * together)
+
+    def part(h, _):
+        for chip in range(n // 2):
+
+            @pl.when(c == chip)
+            def _():
+                attend_visible(
+                    h, streams, together, chip, q_ref, allc_ref, alln_ref, bias_ref, att_ref
+                )
+
+        return slot(h, 0)
+
+    lax.fori_loop(0, steps, part, 0)
+    lax.fori_loop(steps, chunks, slot, 0)
+    returned(chunks - 1)
+
+    def drain(j, _):
+        back_copy(j).wait_send()
+        sib_copy(j).wait_send()
+
+        @pl.when(full_sent(j))
+        def _():
+            full_copy(j).wait_send()
+
+        @pl.when(((c == 1) & (j < near)) | ((c == 2) & (j >= near)))
+        def _():
+            tx_copy(j, 3).wait_send()
+
+        @pl.when((c == 0) & (j >= near))
+        def _():
+            tx_copy(j, 2).wait_send()
+
+        @pl.when((c == 3) & (j < near))
+        def _():
+            relay_copy(j).wait_send()
+
+        return 0
+
+    lax.fori_loop(0, chunks, drain, 0)
+    for d in range(1, n):
+        meta_copy(d).wait_send()
+    for way in (1, 2, 0):
+        own_copy(0, way).wait_send()
+    own_copy(1, 0).wait_send()
+
+    @pl.when(cx > c)
+    def _():
+        own_copy(1, 1).wait_send()
+
+    @pl.when(cy > c)
+    def _():
+        own_copy(1, 2).wait_send()
+
+    @pl.when(c >= 1)
+    def _():
+        pass_copy(0, 0, cx, cy).wait_send()
+
+    @pl.when(c == 3)
+    def _():
+        pass_copy(0, 1, cy, cx).wait_send()
+        pass_copy(1, 1, cy, cx).wait_send()
+
+    @pl.when(c == 1)
+    def _():
+        pass_copy(1, 0, cx, cy).wait_send()
+
+    for chip_ in (cx, cy, cd):
+        forward(0, chip_).wait_send()
+
+        @pl.when(chip_ < c)
+        def _():
+            forward(1, chip_).wait_send()
+
+
+def codes_kernel(mag_ref, nk_ref, code_ref, scale_ref):
+    scale = (mag_ref[...] + 1e-6) / 127.0
+    scale_ref[...] = scale
+    code_ref[...] = (nk_ref[...].astype(F32) / scale).astype(BF16)
+
+
+def fused_body(
+    ssm_input,
+    state_in,
+    state_out,
+    step_size,
+    decay_rate,
+    forget,
+    skip_gain,
+    queries,
+    new_keys,
+    new_values,
+    cache_keys,
+    cache_values,
+    cache_key_scale,
+    cache_value_scale,
+):
+    n = 8
+    tokens, width = ssm_input.shape
+    heads = step_size.shape[1]
+    rows = cache_keys.shape[0]
+    channels = new_keys.shape[1]
+    q_width = queries.shape[1]
+    kv_here = max(1, q_width // ATT_DIM // (ATT_HEADS // KV_HEADS))
+    kvw = kv_here * ATT_DIM
+    groups_here = heads // min(SSM_HEADS // GROUPS, heads)
+    half = width // 2
+    size = min(256, half)
+    chunks = half // size
+    _, fac = factor_rows(tokens)
+    shape = jax.ShapeDtypeStruct
+    dma = pltpu.SemaphoreType.DMA
+    any_ = pl.BlockSpec(memory_space=pl.ANY)
+    piece = pltpu.VMEM((chunks, STATE, size), BF16)
+    y, attended, mag = pl.pallas_call(
+        functools.partial(fused_kernel, chunks),
+        out_shape=(
+            shape((tokens, width), BF16),
+            shape((tokens, q_width), BF16),
+            shape((1, channels), F32),
+        ),
+        in_specs=[any_] * 3 + [VMEM] * 4 + [any_] * 5 + [VMEM] * 2,
+        out_specs=(VMEM,) * 3,
+        scratch_shapes=[
+            pltpu.VMEM((tokens, width), BF16),
+            pltpu.VMEM((tokens, groups_here * STATE), BF16),
+            pltpu.VMEM((tokens, groups_here * STATE), BF16),
+            pltpu.VMEM((tokens, q_width), BF16),
+            pltpu.VMEM((tokens, channels), BF16),
+            pltpu.VMEM((tokens, kvw), BF16),
+            pltpu.VMEM((rows, kvw), BF16),
+            pltpu.VMEM((rows, kvw), BF16),
+            pltpu.VMEM((rows, 2 * kvw), BF16),
+            pltpu.VMEM((tokens, 2 * kvw), BF16),
+            pltpu.VMEM((n, rows, 2 * kvw), BF16),
+            pltpu.VMEM((n, tokens, 2 * kvw), BF16),
+            pltpu.VMEM((tokens, 2 * tokens), F32),
+            pltpu.VMEM((1, channels + 128), F32),
+            pltpu.VMEM((n, 1, channels + 128), F32),
+            pltpu.VMEM((fac, 2 * heads), BF16),
+            pltpu.VMEM((16, 2 * heads), BF16),
+            pltpu.VMEM((tokens, width), BF16),
+            pltpu.VMEM((groups_here, tokens, tokens), BF16),
+            pltpu.VMEM((groups_here, STATE, tokens), BF16),
+            piece,
+            piece,
+            piece,
+            piece,
+            piece,
+            pltpu.VMEM((2, chunks, STATE, size), BF16),
+            pltpu.VMEM((STATE, size), F32),
+            piece,
+            piece,
+            dma((8,)),
+            dma((n,)),
+            dma((n,)),
+            dma((2, 3)),
+            dma((2, n)),
+            dma((2, 4)),
+            dma((2, 2)),
+            dma((chunks,)),
+            dma((chunks,)),
+            dma((3, chunks)),
+            dma((2, chunks)),
+            dma((chunks,)),
+            dma((chunks,)),
+        ],
+        compiler_params=pltpu.CompilerParams(
+            collective_id=0, has_side_effects=True, vmem_limit_bytes=60 * 1024 * 1024
+        ),
+        name="fused",
+    )(
+        ssm_input,
+        state_in,
+        state_out,
+        step_size.T,
+        decay_rate.reshape(1, heads),
+        forget.reshape(1, tokens),
+        skip_gain.reshape(1, heads),
+        queries,
+        new_keys,
+        new_values,
+        cache_keys,
+        cache_values,
+        cache_key_scale.reshape(1, channels),
+        cache_value_scale.reshape(1, channels),
+    )
+    codes, scale = pl.pallas_call(
+        codes_kernel,
+        out_shape=(shape((tokens, channels), BF16), shape((1, channels), F32)),
+        in_specs=[VMEM] * 2,
+        out_specs=(VMEM,) * 2,
+        name="codes",
+    )(mag, new_keys)
+    return (y, attended, codes, scale.reshape(channels))
+
+
+def fits_fused(mesh):
+    heads = SSM_HEADS // mesh.shape["head"]
+    return mesh.shape["seq"] == 8 and heads == 64
+
 
 def solution(mesh):
     in_specs = (
@@ -681,8 +1448,9 @@
         P(),
     )
     out_specs = (P("seq", "head"), P("seq", "head"), P("seq", None), P())
+    general = functools.partial(body, mesh.shape["seq"])
     return jax.shard_map(
-        functools.partial(body, mesh.shape["seq"]),
+        fused_body if fits_fused(mesh) else general,
         mesh=mesh,
         in_specs=in_specs,
         out_specs=out_specs,

time: 76.8 us -> 56.5 us (0.74)
  the two profiles are of different devices: /device:TPU:29 before, /device:TPU:23 now
where the time goes in v1:
time: 56.5 us; the launch traced here: 56.3 us
  Pallas kernels  52 us (92%)
  local copies, waits for them, and re-layouts  3.66 us (6%)
  between operations  0.65 us (1%)
    pallas_call x1, Pallas kernels, fused_body(): pl.pallas_call(functools.partial(fused_kernel, chunks), out_shape=(shape(...  50.2 us
    unnamed x4, local copies, waits for them, and re-layouts  3.66 us
    pallas_call x1, Pallas kernels, fused_body(): pl.pallas_call(codes_kernel, out_shape=(shape((tokens, channels), BF16),...  1.82 us

profile of v1, /device:TPU:23, one launch (start us, length us, event | category | flops | bytes accessed | tf_op | source)
XLA Modules:
  0.0 56.3 jit_solution(8301363345753389862)
XLA Ops:
  0.6 50.2 %fused.1 = (bf16[192,4096]{1,0:T(8,128)(2,1)}, bf16[192,2048]{1,0:T(8,128)(2,1)}, f32[1,1024]{1,0:T(1,128)}) custom-call(bf16[192,4096]{1,0:T(8,128)(2,1)} %x_hbm.1, bf16[192,2048]{1,0:T(8,128)(2,1)} %sin_hbm.1, bf16[192,2048]{1,0:T(8,128)(2,1)} %sout_hbm.1, f32[64,192]{1,0:T(8,128)} %bitcast.7, f32[1,64]{1,0:T(1,128)} %bitcast.11, f32[1,192]{1,0:T(1,128)} %bitcast.10, ...), custom_call_target="tpu_custom_call" | custom-call | tf_op jit(solution)/shard_map/fused/pallas_call | solution.py:1345
  50.9 1.8 %codes.1 = (bf16[192,1024]{1,0:T(8,128)(2,1)}, f32[1,1024]{1,0:T(1,128)}) custom-call(f32[1,1024]{1,0:T(1,128)} %get-tuple-element.11.mag_ref, bf16[192,1024]{1,0:T(8,128)(2,1)} %nk_ref.1), custom_call_target="tpu_custom_call" | custom-call | tf_op jit(solution)/shard_map/codes/pallas_call | solution.py:1418
  52.7 0.0 copy-start
  52.7 2.8 %copy.20 = bf16[192,4096]{1,0:T(8,128)(2,1)} copy(bf16[192,4096]{1,0:T(8,128)(2,1)} %get-tuple-element.18) | data formatting | bytes 3145728
  55.5 0.0 copy-done
  55.5 0.9 %copy.21 = bf16[192,2048]{1,0:T(8,128)(2,1)} copy(bf16[192,2048]{1,0:T(8,128)(2,1)S(1)} %copy-done) | data formatting | bytes 1572864
Async XLA Ops:
  52.7 2.8 %copy-start = (bf16[192,2048]{1,0:T(8,128)(2,1)S(1)}, bf16[192,2048]{1,0:T(8,128)(2,1)}, u32[]{:S(2)}) copy-start(bf16[192,2048]{1,0:T(8,128)(2,1)} %get-tuple-element.19) | copy-start | bytes 2359300

commit v2 on v1

--- a/solution.py
+++ b/solution.py
@@ -743,20 +743,29 @@
     x_hbm,
     sin_hbm,
     sout_hbm,
-    step_ref,
-    decay_ref,
-    forget_ref,
-    skip_ref,
+    step_hbm,
+    decay_hbm,
+    forget_hbm,
+    skip_hbm,
     q_hbm,
     nk_hbm,
     nv_hbm,
     ck_hbm,
     cv_hbm,
-    cks_ref,
-    cvs_ref,
+    cks_hbm,
+    cvs_hbm,
+    y_hbm,
+    att_hbm,
+    mag_hbm,
     y_ref,
     att_ref,
     mag_ref,
+    step_ref,
+    decay_ref,
+    forget_ref,
+    skip_ref,
+    cks_ref,
+    cvs_ref,
     x_ref,
     sin_ref,
     sout_ref,
@@ -787,6 +796,7 @@
     back_ref,
     other_ref,
     load_s,
+    store_s,
     meta_s,
     meta_r,
     kv_s,
@@ -832,23 +842,32 @@
             barrier, inc=1, device_id={"seq": (me + d) % n}, device_id_type=MESH
         )
 
-    loads = [
-        pltpu.make_async_copy(src, dst, load_s.at[k])
-        for k, (src, dst) in enumerate(
-            [
-                (ck_hbm.at[:, cols], ck_ref),
-                (cv_hbm.at[:, cols], cv_ref),
-                (nk_hbm, nk_ref),
-                (nv_hbm.at[:, cols], nv_ref),
-                (sin_hbm.at[:, gcols], sin_ref),
-                (sout_hbm.at[:, gcols], sout_ref),
-                (x_hbm, x_ref),
-                (q_hbm, q_ref),
-            ]
-        )
-    ]
-    for copy in loads:
+    moves = dict(
+        ck=(ck_hbm.at[:, cols], ck_ref),
+        cks=(cks_hbm.at[:, cols], cks_ref),
+        cv=(cv_hbm.at[:, cols], cv_ref),
+        cvs=(cvs_hbm.at[:, cols], cvs_ref),
+        nv=(nv_hbm.at[:, cols], nv_ref),
+        nk=(nk_hbm, nk_ref),
+        step=(step_hbm, step_ref),
+        decay=(decay_hbm, decay_ref),
+        forget=(forget_hbm, forget_ref),
+        skip=(skip_hbm, skip_ref),
+        sin=(sin_hbm.at[:, gcols], sin_ref),
+        sout=(sout_hbm.at[:, gcols], sout_ref),
+        x=(x_hbm, x_ref),
+        q=(q_hbm, q_ref),
+    )
+    loads = {
+        name: pltpu.make_async_copy(src, dst, load_s.at[k])
+        for k, (name, (src, dst)) in enumerate(moves.items())
+    }
+    for copy in loads.values():
         copy.start()
+
+    def ready(*names):
+        for name in names:
+            loads[name].wait()
 
     def remote(src, dst, ssem, rsem, to):
         return pltpu.make_async_remote_copy(
@@ -897,15 +916,13 @@
             owns[kind], alls[kind].at[slot], kv_s.at[kind, 0], kv_r.at[kind, slot], other
         ).wait_recv()
 
-    loads[0].wait()
-    loads[1].wait()
-    kvc_ref[:, :kvw] = (ck_ref[...].astype(F32) * cks_ref[:, cols]).astype(BF16)
-    kvc_ref[:, kvw:] = (cv_ref[...].astype(F32) * cvs_ref[:, cols]).astype(BF16)
+    ready("ck", "cks", "cv", "cvs")
+    kvc_ref[:, :kvw] = (ck_ref[...].astype(F32) * cks_ref[...]).astype(BF16)
+    kvc_ref[:, kvw:] = (cv_ref[...].astype(F32) * cvs_ref[...]).astype(BF16)
     pl.semaphore_wait(barrier, n - 1)
     for way in (1, 2, 0):
         own_copy(0, way).start()
-    loads[2].wait()
-    loads[3].wait()
+    ready("nv", "nk")
     kvn_ref[:, :kvw] = nk_ref[:, cols]
     kvn_ref[:, kvw:] = nv_ref[...]
 
@@ -922,6 +939,7 @@
     row, col = iota((tokens, tokens), 0), iota((tokens, tokens), 1)
     lower = jnp.where(col <= row, 1.0, 0.0)
     eye = jnp.where(col == row, 1.0, 0.0).astype(BF16)
+    ready("step", "decay", "forget", "skip")
     step = step_ref[...].T
     forgotten = jnp.sum(lower * forget_ref[...], axis=1, keepdims=True)
     decayed = jnp.dot(
@@ -963,8 +981,7 @@
     )
     put("skip", skip_ref[...])
     put("fade", jnp.exp2(running))
-    loads[4].wait()
-    loads[5].wait()
+    ready("sin", "sout")
     for g in range(groups_here):
         gc = slice(g * STATE, (g + 1) * STATE)
         maps_in = sin_ref[:, gc]
@@ -975,7 +992,7 @@
         turned_ref[g] = lax.dot_general(
             maps_in, eye, (((0,), (0,)), ((), ())), preferred_element_type=F32
         ).astype(BF16)
-    loads[6].wait()
+    ready("x")
 
     def spread(first, final, begin):
         rows = fac_ref[places[first][0] : places[final][1]]
@@ -1002,7 +1019,24 @@
         sib_copy(j).start()
         return 0
 
+    def pass_cache():
+        arrived(0, dev(cx))
+
+        @pl.when(c >= 1)
+        def _():
+            pass_copy(0, 0, cx, cy).start()
+
+        forward(0, cx).start()
+        arrived(0, dev(cy))
+
+        @pl.when(c == 3)
+        def _():
+            pass_copy(0, 1, cy, cx).start()
+
+        forward(0, cy).start()
+
     lax.fori_loop(0, chunks, give, 0)
+    pass_cache()
     meta_arrived(other)
 
     def logs_of(r):
@@ -1047,23 +1081,6 @@
 
     lax.fori_loop(0, chunks, own, 0)
 
-    def pass_cache():
-        arrived(0, dev(cx))
-
-        @pl.when(c >= 1)
-        def _():
-            pass_copy(0, 0, cx, cy).start()
-
-        forward(0, cx).start()
-        arrived(0, dev(cy))
-
-        @pl.when(c == 3)
-        def _():
-            pass_copy(0, 1, cy, cx).start()
-
-        forward(0, cy).start()
-
-    pass_cache()
     bias_ref[...] = jnp.where(
         iota((tokens, 2 * tokens), 1) <= i * tokens + iota((tokens, 2 * tokens), 0), 0.0, NEG
     )
@@ -1090,10 +1107,7 @@
         y_ref[:, here] = (y + by[at + tokens : at + tokens + 1] * x).astype(BF16)
         return 0
 
-    lax.fori_loop(0, 2 * chunks, within, 0)
-
-    arrived(0, dev(cd))
-    forward(0, cd).start()
+    lax.fori_loop(0, chunks, within, 0)
 
     @pl.when(cx < c)
     def _():
@@ -1115,6 +1129,10 @@
 
         forward(1, cy).start()
 
+    lax.fori_loop(chunks, 2 * chunks, within, 0)
+    arrived(0, dev(cd))
+    forward(0, cd).start()
+
     for d in range(1, n):
         r = (me + d) % n
 
@@ -1125,6 +1143,8 @@
     chip = jnp.where(c == 0, 1, jnp.where(c == 3, 2, c))
     set_fades(logs_of(2 * chip) + logs_of(2 * chip + 1))
     mag_ref[...] = jnp.max(allm_ref[:, 0, :channels], axis=0, keepdims=True)
+    mag_out = pltpu.make_async_copy(mag_ref, mag_hbm, store_s.at[2 * chunks])
+    mag_out.start()
 
     @pl.when(cd < c)
     def _():
@@ -1143,11 +1163,14 @@
         def _():
             arrived(1, there * 2 + 1 - i)
 
-    loads[7].wait()
+    ready("q")
 
     def order(s):
-        left = (1 - c // 2) * ((s + near) % chunks) + (c // 2) * (near * (1 - s % 2) + s // 2)
-        return (c % 2) * s + (1 - c % 2) * left
+        return (s + (1 - c % 2) * near) % chunks
+
+    def y_out(k):
+        here = lanes(k * size, size)
+        return pltpu.make_async_copy(y_ref.at[:, here], y_hbm.at[:, here], store_s.at[k])
 
     def prior(begin, carried):
         here = lanes(begin, size)
@@ -1155,6 +1178,7 @@
         term = jnp.dot(sout_ref[:, lanes(group * STATE, STATE)], carried, preferred_element_type=F32)
         by = spread("fade", "fade", begin)
         y_ref[:, here] = (y_ref[:, here].astype(F32) + by * term).astype(BF16)
+        y_out(begin // size).start()
 
     def rx_wait(slot, j):
         remote(
@@ -1242,6 +1266,8 @@
         return slot(h, 0)
 
     lax.fori_loop(0, steps, part, 0)
+    att_out = pltpu.make_async_copy(att_ref, att_hbm, store_s.at[2 * chunks + 1])
+    att_out.start()
     lax.fori_loop(steps, chunks, slot, 0)
     returned(chunks - 1)
 
@@ -1268,6 +1294,14 @@
         return 0
 
     lax.fori_loop(0, chunks, drain, 0)
+
+    def stored(k, _):
+        y_out(k).wait()
+        return 0
+
+    lax.fori_loop(0, 2 * chunks, stored, 0)
+    mag_out.wait()
+    att_out.wait()
     for d in range(1, n):
         meta_copy(d).wait_send()
     for way in (1, 2, 0):
@@ -1303,10 +1337,39 @@
             forward(1, chip_).wait_send()
 
 
-def codes_kernel(mag_ref, nk_ref, code_ref, scale_ref):
+def finish_kernel(
+    y_hbm, att_hbm, mag_hbm, nk_hbm, yo_hbm, atto_hbm, code_hbm, scale_ref,
+    y_ref, att_ref, mag_ref, nk_ref, code_ref, in_s, out_s,
+):
+    pieces = 4
+    wide, slim = y_ref.shape[0] // pieces, att_ref.shape[0] // pieces
+    mag_in = pltpu.make_async_copy(mag_hbm, mag_ref, in_s.at[2 * pieces])
+    nk_in = pltpu.make_async_copy(nk_hbm, nk_ref, in_s.at[2 * pieces + 1])
+    code_out = pltpu.make_async_copy(code_ref, code_hbm, out_s.at[2 * pieces])
+    ins, outs = [], []
+    for p in range(pieces):
+        for k, (src, mid, dst, rows) in enumerate(
+            [(y_hbm, y_ref, yo_hbm, wide), (att_hbm, att_ref, atto_hbm, slim)]
+        ):
+            at = pl.ds(p * rows, rows)
+            ins.append(pltpu.make_async_copy(src.at[at], mid.at[at], in_s.at[2 * p + k]))
+            outs.append(pltpu.make_async_copy(mid.at[at], dst.at[at], out_s.at[2 * p + k]))
+    mag_in.start()
+    nk_in.start()
+    for copy in ins:
+        copy.start()
+    mag_in.wait()
+    nk_in.wait()
     scale = (mag_ref[...] + 1e-6) / 127.0
     scale_ref[...] = scale
     code_ref[...] = (nk_ref[...].astype(F32) / scale).astype(BF16)
+    code_out.start()
+    for a, b in zip(ins, outs):
+        a.wait()
+        b.start()
+    code_out.wait()
+    for b in outs:
+        b.wait()
 
 
 def fused_body(
@@ -1349,9 +1412,18 @@
             shape((tokens, q_width), BF16),
             shape((1, channels), F32),
         ),
-        in_specs=[any_] * 3 + [VMEM] * 4 + [any_] * 5 + [VMEM] * 2,
-        out_specs=(VMEM,) * 3,
+        in_specs=[any_] * 14,
+        out_specs=(any_,) * 3,
         scratch_shapes=[
+            pltpu.VMEM((tokens, width), BF16),
+            pltpu.VMEM((tokens, q_width), BF16),
+            pltpu.VMEM((1, channels), F32),
+            pltpu.VMEM((heads, tokens), F32),
+            pltpu.VMEM((1, heads), F32),
+            pltpu.VMEM((1, tokens), F32),
+            pltpu.VMEM((1, heads), F32),
+            pltpu.VMEM((1, kvw), F32),
+            pltpu.VMEM((1, kvw), F32),
             pltpu.VMEM((tokens, width), BF16),
             pltpu.VMEM((tokens, groups_here * STATE), BF16),
             pltpu.VMEM((tokens, groups_here * STATE), BF16),
@@ -1381,7 +1453,8 @@
             pltpu.VMEM((STATE, size), F32),
             piece,
             piece,
-            dma((8,)),
+            dma((14,)),
+            dma((2 * chunks + 2,)),
             dma((n,)),
             dma((n,)),
             dma((2, 3)),
@@ -1415,13 +1488,27 @@
         cache_key_scale.reshape(1, channels),
         cache_value_scale.reshape(1, channels),
     )
-    codes, scale = pl.pallas_call(
-        codes_kernel,
-        out_shape=(shape((tokens, channels), BF16), shape((1, channels), F32)),
-        in_specs=[VMEM] * 2,
-        out_specs=(VMEM,) * 2,
-        name="codes",
-    )(mag, new_keys)
+    y, attended, codes, scale = pl.pallas_call(
+        finish_kernel,
+        out_shape=(
+            shape((tokens, width), BF16),
+            shape((tokens, q_width), BF16),
+            shape((tokens, channels), BF16),
+            shape((1, channels), F32),
+        ),
+        in_specs=[any_] * 4,
+        out_specs=(any_,) * 3 + (VMEM,),
+        scratch_shapes=[
+            pltpu.VMEM((tokens, width), BF16),
+            pltpu.VMEM((tokens, q_width), BF16),
+            pltpu.VMEM((1, channels), F32),
+            pltpu.VMEM((tokens, channels), BF16),
+            pltpu.VMEM((tokens, channels), BF16),
+            dma((10,)),
+            dma((9,)),
+        ],
+        name="finish",
+    )(y, attended, mag, new_keys)
     return (y, attended, codes, scale.reshape(channels))
 
 

time: 56.5 us -> 47.2 us (0.84)
  the two profiles are of different devices: /device:TPU:23 before, /device:TPU:29 now
where the time goes in v2:
time: 47.2 us; the launch traced here: 47 us
  Pallas kernels  46.3 us (98%)
  between operations  0.64 us (1%)
    pallas_call x1, Pallas kernels, fused_body(): pl.pallas_call(functools.partial(fused_kernel, chunks), out_shape=(shape(...  43 us
    pallas_call x1, Pallas kernels, fused_body(): pl.pallas_call(finish_kernel, out_shape=(shape((tokens, width), BF16), sh...  3.34 us

profile of v2, /device:TPU:29, one launch (start us, length us, event | category | flops | bytes accessed | tf_op | source)
XLA Modules:
  0.0 47.0 jit_solution(18029226453349294334)
XLA Ops:
  0.6 43.0 %fused.1 = (bf16[192,4096]{1,0:T(8,128)(2,1)}, bf16[192,2048]{1,0:T(8,128)(2,1)}, f32[1,1024]{1,0:T(1,128)}) custom-call(bf16[192,4096]{1,0:T(8,128)(2,1)} %x_hbm.1, bf16[192,2048]{1,0:T(8,128)(2,1)} %sin_hbm.1, bf16[192,2048]{1,0:T(8,128)(2,1)} %sout_hbm.1, f32[64,192]{1,0:T(8,128)} %bitcast.7, f32[1,64]{1,0:T(1,128)} %bitcast.11, f32[1,192]{1,0:T(1,128)} %bitcast.10, ...), custom_call_target="tpu_custom_call" | custom-call | tf_op jit(solution)/shard_map/fused/pallas_call | solution.py:1408
  43.6 3.3 %finish.1 = (bf16[192,4096]{1,0:T(8,128)(2,1)}, bf16[192,2048]{1,0:T(8,128)(2,1)}, bf16[192,1024]{1,0:T(8,128)(2,1)}, f32[1,1024]{1,0:T(1,128)}) custom-call(bf16[192,4096]{1,0:T(8,128)(2,1)} %get-tuple-element.11.y_hbm, bf16[192,2048]{1,0:T(8,128)(2,1)} %get-tuple-element.12.att_hbm, f32[1,1024]{1,0:T(1,128)} %get-tuple-element.13.mag_hbm, ...), custom_call_target="tpu_custom_call" | custom-call | tf_op jit(solution)/shard_map/finish/pallas_call | solution.py:1491

commit v3 on v2

--- a/solution.py
+++ b/solution.py
@@ -699,40 +699,75 @@
     return jnp.concatenate([v, jnp.ones(v.shape, BF16)], axis=1)
 
 
-def attend_visible(step, streams, together, chip, q_ref, allc_ref, alln_ref, bias_ref, att_ref):
+NT = (((1,), (1,)), ((), ()))
+FACTOR = ATT_DIM**-0.5 * LOG2E
+
+
+def stream_heads(step, streams, together):
+    first = step * streams * together
+    return [
+        [lanes((first + e * together + f) * ATT_DIM, ATT_DIM) for f in range(together)]
+        for e in range(streams)
+    ]
+
+
+def key_columns(step, streams, together, q_ref, all_ref):
+    kvw = all_ref.shape[2] // 2
+    share = (q_ref.shape[1] // ATT_DIM) // (kvw // ATT_DIM)
+    k = (step * streams * together) // share
+    return lanes(k * ATT_DIM, ATT_DIM), lanes(kvw + k * ATT_DIM, ATT_DIM)
+
+
+def score_streams(own, q_ref, keys):
+    return [
+        lax.dot_general(
+            jnp.concatenate([q_ref[:, o] for o in heads], axis=0),
+            keys,
+            NT,
+            preferred_element_type=F32,
+        )
+        for heads in own
+    ]
+
+
+def attend_cache(step, streams, together, q_ref, allc_ref, sum_ref, peak_ref):
+    rows = together * q_ref.shape[0]
+    at, av = key_columns(step, streams, together, q_ref, allc_ref)
+    keys = allc_ref[:, :, at].reshape(-1, ATT_DIM)
+    values = with_ones(allc_ref[:, :, av].reshape(-1, ATT_DIM))
+    own = stream_heads(step, streams, together)
+    scores = score_streams(own, q_ref, keys)
+    for e in range(streams):
+        peak = jnp.max(scores[e], axis=1, keepdims=True)
+        p = jnp.exp2((scores[e] - peak) * FACTOR).astype(BF16)
+        here = pl.ds(pl.multiple_of((step * streams + e) * rows, rows), rows)
+        sum_ref[here, :] = jnp.dot(p, values, preferred_element_type=F32)
+        peak_ref[here, :] = jnp.broadcast_to(peak, (rows, 128))
+
+
+def attend_span(
+    step, streams, together, chip, q_ref, alln_ref, bias_ref, sum_ref, peak_ref, att_ref
+):
     tokens = q_ref.shape[0]
-    kvw = allc_ref.shape[2] // 2
-    share = (q_ref.shape[1] // ATT_DIM) // (kvw // ATT_DIM)
-    factor = ATT_DIM**-0.5 * LOG2E
-    nt = (((1,), (1,)), ((), ()))
-    k = (step * streams * together) // share
-    at, av = lanes(k * ATT_DIM, ATT_DIM), lanes(kvw + k * ATT_DIM, ATT_DIM)
+    rows = together * tokens
+    at, av = key_columns(step, streams, together, q_ref, alln_ref)
     seen = 2 * chip + 2
-
-    def rows_of(cols):
-        return jnp.concatenate(
-            [
-                allc_ref[:, :, cols].reshape(-1, ATT_DIM),
-                alln_ref[:seen, :, cols].reshape(-1, ATT_DIM),
-            ],
-            axis=0,
-        )
-
-    keys, values = rows_of(at), with_ones(rows_of(av))
+    keys = alln_ref[:seen, :, at].reshape(-1, ATT_DIM)
+    values = with_ones(alln_ref[:seen, :, av].reshape(-1, ATT_DIM))
     free = keys.shape[0] - 2 * tokens
-    own, scores = [], []
-    for e in range(streams):
-        first = (step * streams + e) * together
-        own.append([lanes((first + f) * ATT_DIM, ATT_DIM) for f in range(together)])
-        q = jnp.concatenate([q_ref[:, o] for o in own[e]], axis=0)
-        scores.append(lax.dot_general(q, keys, nt, preferred_element_type=F32))
+    own = stream_heads(step, streams, together)
+    scores = score_streams(own, q_ref, keys)
     bias = bias_ref[...]
     for e in range(streams):
         near = scores[e][:, free:].reshape(together, tokens, -1) + bias[None]
-        s = jnp.concatenate([scores[e][:, :free], near.reshape(together * tokens, -1)], axis=1)
-        peak = jnp.max(s, axis=1, keepdims=True)
-        p = jnp.exp2((s - peak) * factor).astype(BF16)
+        near = near.reshape(rows, -1)
+        s = jnp.concatenate([scores[e][:, :free], near], axis=1) if free else near
+        here = pl.ds(pl.multiple_of((step * streams + e) * rows, rows), rows)
+        before = peak_ref[here, :][:, :1]
+        peak = jnp.maximum(before, jnp.max(s, axis=1, keepdims=True))
+        p = jnp.exp2((s - peak) * FACTOR).astype(BF16)
         both = jnp.dot(p, values, preferred_element_type=F32)
+        both += sum_ref[here, :] * jnp.exp2((before - peak) * FACTOR)
         result = (both[:, :ATT_DIM] / both[:, ATT_DIM:]).astype(BF16)
         for f, o in enumerate(own[e]):
             att_ref[:, o] = result[f * tokens : (f + 1) * tokens]
@@ -795,6 +830,10 @@
     enter_ref,
     back_ref,
     other_ref,
+    sum_ref,
+    peak_ref,
+    pick_ref,
+    carry_ref,
     load_s,
     store_s,
     meta_s,
@@ -819,7 +858,8 @@
     kvw = kvc_ref.shape[1] // 2
     half = width // 2
     size = half // chunks
-    near = chunks // 2
+    near = chunks * 3 // 8
+    mid = chunks // 2
     places, _ = factor_rows(tokens)
     nb = span_blocks(tokens)
     bs = tokens // nb
@@ -916,6 +956,8 @@
             owns[kind], alls[kind].at[slot], kv_s.at[kind, 0], kv_r.at[kind, slot], other
         ).wait_recv()
 
+    for k in range(width // 512):
+        pick_ref[:, k * 512 : (k + 1) * 512] = choose2(heads, k * 512, 512)
     ready("ck", "cks", "cv", "cvs")
     kvc_ref[:, :kvw] = (ck_ref[...].astype(F32) * cks_ref[...]).astype(BF16)
     kvc_ref[:, kvw:] = (cv_ref[...].astype(F32) * cvs_ref[...]).astype(BF16)
@@ -994,29 +1036,31 @@
         ).astype(BF16)
     ready("x")
 
-    def spread(first, final, begin):
+    def spread(first, final, begin, wide=size):
         rows = fac_ref[places[first][0] : places[final][1]]
-        return jnp.dot(rows, choose2(heads, begin, size), preferred_element_type=F32)
+        return jnp.dot(rows, pick_ref[:, lanes(begin, wide)], preferred_element_type=F32)
 
     def local_state(begin):
-        here = lanes(begin, size)
-        by = spread("z", "tail", begin)
+        here = lanes(begin, 2 * size)
+        by = spread("z", "tail", begin, 2 * size)
         scaled = (x_ref[:, here].astype(F32) * by[:tokens]).astype(BF16)
         z_ref[:, here] = scaled
         sums = jnp.dot(
             turned_ref[begin // (per_group * HEAD_DIM)], scaled, preferred_element_type=F32
         )
-        return (sums * by[tokens : tokens + 1]).astype(BF16)
+        sums = (sums * by[tokens : tokens + 1]).astype(BF16)
+        return sums[:, :size], sums[:, size:]
 
     def sib_copy(j):
         return remote(give_ref.at[j], sib_ref.at[j], sib_s.at[j], sib_r.at[j], other)
 
-    shift = (c % 2) * (1 - c // 2) * near
+    shift = (c % 2) * (1 - c // 2) * mid
 
     def give(s, _):
-        j = (s + shift) % chunks
-        give_ref[j] = local_state((1 - i) * half + j * size)
-        sib_copy(j).start()
+        j = (2 * s + shift) % chunks
+        for e, state in enumerate(local_state((1 - i) * half + j * size)):
+            give_ref[j + e] = state
+            sib_copy(j + e).start()
         return 0
 
     def pass_cache():
@@ -1035,7 +1079,7 @@
 
         forward(0, cy).start()
 
-    lax.fori_loop(0, chunks, give, 0)
+    lax.fori_loop(0, chunks // 2, give, 0)
     pass_cache()
     meta_arrived(other)
 
@@ -1050,7 +1094,9 @@
 
     def fades(j):
         return jnp.dot(
-            fade_ref[...], choose2(heads, i * half + j * size, size), preferred_element_type=F32
+            fade_ref[...],
+            pick_ref[:, lanes(i * half + j * size, size)],
+            preferred_element_type=F32,
         )
 
     set_fades(jnp.zeros((1, heads), F32))
@@ -1065,30 +1111,35 @@
         return (c == 0) | ((c == 1) & (j >= near)) | ((c == 2) & (j < near))
 
     def own(s, _):
-        j = (s + shift) % chunks
-        mine = local_state(i * half + j * size)
-        mine_ref[j] = mine
-        sib_copy(j).wait_recv()
-        mine, theirs = mine.astype(F32), sib_ref[j].astype(F32)
-        d1 = fades(j)[1:2]
-        full_ref[j] = jnp.where(i == 0, d1 * mine + theirs, d1 * theirs + mine).astype(BF16)
-
-        @pl.when(full_sent(j))
-        def _():
-            full_copy(j).start()
+        j = (2 * s + shift) % chunks
+        states = local_state(i * half + j * size)
+        for e, mine in enumerate(states):
+            mine_ref[j + e] = mine
+        for e in range(2):
+            sib_copy(j + e).wait_recv()
+        for e, mine in enumerate(states):
+            mine, theirs = mine.astype(F32), sib_ref[j + e].astype(F32)
+            d1 = fades(j + e)[1:2]
+            full = jnp.where(i == 0, d1 * mine + theirs, d1 * theirs + mine)
+            full_ref[j + e] = full.astype(BF16)
+
+        for e in range(2):
+
+            @pl.when(full_sent(j + e))
+            def _():
+                full_copy(j + e).start()
 
         return 0
 
-    lax.fori_loop(0, chunks, own, 0)
-
+    lax.fori_loop(0, chunks // 2, own, 0)
     bias_ref[...] = jnp.where(
         iota((tokens, 2 * tokens), 1) <= i * tokens + iota((tokens, 2 * tokens), 0), 0.0, NEG
     )
 
     def within(s, _):
-        begin = s * size
-        here = lanes(begin, size)
-        by = spread("z0" if nb > 1 else "out", "skip", begin)
+        begin = s * 2 * size
+        here = lanes(begin, 2 * size)
+        by = spread("z0" if nb > 1 else "out", "skip", begin, 2 * size)
         at = 0
         gram = gram_ref[begin // (per_group * HEAD_DIM)]
         x = x_ref[:, here].astype(F32)
@@ -1107,8 +1158,6 @@
         y_ref[:, here] = (y + by[at + tokens : at + tokens + 1] * x).astype(BF16)
         return 0
 
-    lax.fori_loop(0, chunks, within, 0)
-
     @pl.when(cx < c)
     def _():
         arrived(1, dev(cx))
@@ -1129,9 +1178,10 @@
 
         forward(1, cy).start()
 
-    lax.fori_loop(chunks, 2 * chunks, within, 0)
+    lax.fori_loop(0, chunks // 2, within, 0)
     arrived(0, dev(cd))
     forward(0, cd).start()
+    lax.fori_loop(chunks // 2, chunks, within, 0)
 
     for d in range(1, n):
         r = (me + d) % n
@@ -1146,27 +1196,39 @@
     mag_out = pltpu.make_async_copy(mag_ref, mag_hbm, store_s.at[2 * chunks])
     mag_out.start()
 
-    @pl.when(cd < c)
-    def _():
-        arrived(1, dev(cd))
-        forward(1, cd).start()
-
     allc_ref[me] = kvc_ref[...]
     alln_ref[me] = kvn_ref[...]
     arrived(0, other)
-    arrived(1, other)
     for d in range(1, 4):
-        there = (c + d) % 4
-        arrived(0, there * 2 + 1 - i)
-
-        @pl.when(there < c)
-        def _():
-            arrived(1, there * 2 + 1 - i)
+        arrived(0, (c + d) % 4 * 2 + 1 - i)
 
     ready("q")
 
+    def span_arrived():
+        @pl.when(cd < c)
+        def _():
+            arrived(1, dev(cd))
+            forward(1, cd).start()
+
+        arrived(1, other)
+        for d in range(1, 4):
+            there = (c + d) % 4
+
+            @pl.when(there < c)
+            def _():
+                arrived(1, there * 2 + 1 - i)
+
+    def second_way(s):
+        late = s // mid
+        return mid + s - late * (2 * mid - near)
+
     def order(s):
-        return (s + (1 - c % 2) * near) % chunks
+        later = s // (chunks - near)
+        even = (1 - later) * second_way(s * (1 - later)) + later * (s - chunks + near)
+        last = (s + chunks - near) // chunks
+        odd = (1 - last) * s + last * second_way((s - near) * last)
+        third = c // 2
+        return (1 - c % 2) * even + (c % 2) * (third * odd + (1 - third) * s)
 
     def y_out(k):
         here = lanes(k * size, size)
@@ -1177,7 +1239,11 @@
         group = begin // (per_group * HEAD_DIM)
         term = jnp.dot(sout_ref[:, lanes(group * STATE, STATE)], carried, preferred_element_type=F32)
         by = spread("fade", "fade", begin)
-        y_ref[:, here] = (y_ref[:, here].astype(F32) + by * term).astype(BF16)
+        return begin, (y_ref[:, here].astype(F32) + by * term).astype(BF16)
+
+    def put_prior(result):
+        begin, value = result
+        y_ref[:, lanes(begin, size)] = value
         y_out(begin // size).start()
 
     def rx_wait(slot, j):
@@ -1196,37 +1262,59 @@
     def back_copy(j):
         return remote(back_ref.at[j], other_ref.at[j], back_s.at[j], back_r.at[j], other)
 
-    def combine(s):
+    def pass_on(s):
+        @pl.when((c == 1) | (c == 2))
+        def _():
+            j = (c % 2) * s + (1 - c % 2) * second_way(s)
+            rx_wait(0, j)
+            keep = fades(j)[2:3]
+            tx_ref[j] = (keep * rx_ref[0, j].astype(F32) + full_ref[j].astype(F32)).astype(BF16)
+            tx_copy(j, 3).start()
+
+        @pl.when(c == 0)
+        def _():
+            j = second_way(s)
+            rx_wait(1, j)
+            keep = fades(j)[2:3]
+            tx_ref[j] = (keep * full_ref[j].astype(F32) + rx_ref[1, j].astype(F32)).astype(BF16)
+            tx_copy(j, 2).start()
+
+        @pl.when(c == 3)
+        def _():
+            rx_wait(0, s)
+            relay_copy(s).start()
+
+    base = 2 + (c // 2) * (4 + c % 2)
+    stride = 1 + (c % 2) * (1 - c // 2)
+    passes = (c % 2) * near + (1 - c % 2) * (chunks - near)
+
+    def pass_at(place):
+        ahead = place - base
+        s = ahead // stride
+
+        @pl.when((ahead >= 0) & (ahead % stride == 0) & (s < passes))
+        def _():
+            pass_on(s)
+
+    def settle(s):
         j = order(s)
         by = fades(j)
         d0, keep = by[0:1], by[2:3]
 
-        @pl.when(c > 0)
+        @pl.when((c > 0) & (s >= passes))
         def _():
             rx_wait(0, j)
 
-        @pl.when((c == 3) & (j < near))
-        def _():
-            relay_copy(j).start()
+        @pl.when((c == 3) & (s < near))
+        def _():
             rx_wait(1, j)
             enter_ref[...] = keep * rx_ref[0, j].astype(F32) + rx_ref[1, j].astype(F32)
 
-        @pl.when(((c == 1) & (j < near)) | ((c == 2) & (j >= near)))
-        def _():
-            tx_ref[j] = (keep * rx_ref[0, j].astype(F32) + full_ref[j].astype(F32)).astype(BF16)
-            tx_copy(j, 3).start()
-
-        @pl.when((c == 0) & (j >= near))
-        def _():
-            rx_wait(1, j)
-            tx_ref[j] = (keep * full_ref[j].astype(F32) + rx_ref[1, j].astype(F32)).astype(BF16)
-            tx_copy(j, 2).start()
-
         @pl.when(c == 0)
         def _():
             enter_ref[...] = jnp.zeros(enter_ref.shape, F32)
 
-        @pl.when((c == 1) | (c == 2) | ((c == 3) & (j >= near)))
+        @pl.when((c == 1) | (c == 2) | ((c == 3) & (s >= near)))
         def _():
             enter_ref[...] = rx_ref[0, j].astype(F32)
 
@@ -1235,41 +1323,68 @@
         middle = d0 * enter + first
         back_ref[j] = jnp.where(i == 0, middle, enter).astype(BF16)
         back_copy(j).start()
-        prior(i * half + j * size, jnp.where(i == 0, enter, middle).astype(BF16))
-
-    def returned(s):
-        j = order(s)
-        back_copy(j).wait_recv()
-        prior((1 - i) * half + j * size, other_ref[j])
+        carry_ref[...] = jnp.where(i == 0, enter, middle).astype(BF16)
 
     def slot(s, _):
-        combine(s)
+        settle(s)
+
+        @pl.when(s == 0)
+        def _():
+            put_prior(prior(i * half + order(s) * size, carry_ref[...]))
 
         @pl.when(s > 0)
         def _():
-            returned(s - 1)
+            far = order(s - 1)
+            back_copy(far).wait_recv()
+            both = [
+                prior(i * half + order(s) * size, carry_ref[...]),
+                prior((1 - i) * half + far * size, other_ref[far]),
+            ]
+            for each in both:
+                put_prior(each)
 
         return 0
 
-    streams, together = 2, 2
+    streams, together = 4, 1
     steps = q_heads // (streams * together)
-
-    def part(h, _):
+    pass_at(2)
+
+    def first_part(h, _):
+        attend_cache(h, streams, together, q_ref, allc_ref, sum_ref, peak_ref)
+        pass_at(3 + h)
+        return 0
+
+    lax.fori_loop(0, steps, first_part, 0)
+    span_arrived()
+
+    def second_part(h, _):
         for chip in range(n // 2):
 
             @pl.when(c == chip)
             def _():
-                attend_visible(
-                    h, streams, together, chip, q_ref, allc_ref, alln_ref, bias_ref, att_ref
+                attend_span(
+                    h,
+                    streams,
+                    together,
+                    chip,
+                    q_ref,
+                    alln_ref,
+                    bias_ref,
+                    sum_ref,
+                    peak_ref,
+                    att_ref,
                 )
 
+        pass_at(3 + steps + h)
         return slot(h, 0)
 
-    lax.fori_loop(0, steps, part, 0)
+    lax.fori_loop(0, steps, second_part, 0)
     att_out = pltpu.make_async_copy(att_ref, att_hbm, store_s.at[2 * chunks + 1])
     att_out.start()
     lax.fori_loop(steps, chunks, slot, 0)
-    returned(chunks - 1)
+    far = order(chunks - 1)
+    back_copy(far).wait_recv()
+    put_prior(prior((1 - i) * half + far * size, other_ref[far]))
 
     def drain(j, _):
         back_copy(j).wait_send()
@@ -1453,6 +1568,10 @@
             pltpu.VMEM((STATE, size), F32),
             piece,
             piece,
+            pltpu.VMEM((q_width // ATT_DIM * tokens, 2 * ATT_DIM), F32),
+            pltpu.VMEM((q_width // ATT_DIM * tokens, 128), F32),
+            pltpu.VMEM((2 * heads, width), BF16),
+            pltpu.VMEM((STATE, size), BF16),
             dma((14,)),
             dma((2 * chunks + 2,)),
             dma((n,)),

time: 47.2 us -> 43.8 us (0.928)
  the two profiles are of different devices: /device:TPU:29 before, /device:TPU:23 now
where the time goes in v3:
time: 43.8 us; the launch traced here: 43.3 us
  Pallas kernels  42.7 us (97%)
  between operations  0.64 us (1%)
    pallas_call x1, Pallas kernels, fused_body(): pl.pallas_call(functools.partial(fused_kernel, chunks), out_shape=(shape(...  39.4 us
    pallas_call x1, Pallas kernels, fused_body(): pl.pallas_call(finish_kernel, out_shape=(shape((tokens, width), BF16), sh...  3.34 us

profile of v3, /device:TPU:23, one launch (start us, length us, event | category | flops | bytes accessed | tf_op | source)
XLA Modules:
  0.0 43.3 jit_solution(4616950374484144627)
XLA Ops:
  0.6 39.4 %fused.1 = (bf16[192,4096]{1,0:T(8,128)(2,1)}, bf16[192,2048]{1,0:T(8,128)(2,1)}, f32[1,1024]{1,0:T(1,128)}) custom-call(bf16[192,4096]{1,0:T(8,128)(2,1)} %x_hbm.1, bf16[192,2048]{1,0:T(8,128)(2,1)} %sin_hbm.1, bf16[192,2048]{1,0:T(8,128)(2,1)} %sout_hbm.1, f32[64,192]{1,0:T(8,128)} %bitcast.7, f32[1,64]{1,0:T(1,128)} %bitcast.11, f32[1,192]{1,0:T(1,128)} %bitcast.10, ...), custom_call_target="tpu_custom_call" | custom-call | tf_op jit(solution)/shard_map/fused/pallas_call | solution.py:1523
  40.0 3.3 %finish.1 = (bf16[192,4096]{1,0:T(8,128)(2,1)}, bf16[192,2048]{1,0:T(8,128)(2,1)}, bf16[192,1024]{1,0:T(8,128)(2,1)}, f32[1,1024]{1,0:T(1,128)}) custom-call(bf16[192,4096]{1,0:T(8,128)(2,1)} %get-tuple-element.11.y_hbm, bf16[192,2048]{1,0:T(8,128)(2,1)} %get-tuple-element.12.att_hbm, f32[1,1024]{1,0:T(1,128)} %get-tuple-element.13.mag_hbm, ...), custom_call_target="tpu_custom_call" | custom-call | tf_op jit(solution)/shard_map/finish/pallas_call | solution.py:1610

commit v4 on v3

--- a/solution.py
+++ b/solution.py
@@ -789,12 +789,10 @@
     cv_hbm,
     cks_hbm,
     cvs_hbm,
-    y_hbm,
-    att_hbm,
-    mag_hbm,
     y_ref,
     att_ref,
-    mag_ref,
+    code_ref,
+    scale_ref,
     step_ref,
     decay_ref,
     forget_ref,
@@ -835,7 +833,6 @@
     pick_ref,
     carry_ref,
     load_s,
-    store_s,
     meta_s,
     meta_r,
     kv_s,
@@ -1192,9 +1189,9 @@
 
     chip = jnp.where(c == 0, 1, jnp.where(c == 3, 2, c))
     set_fades(logs_of(2 * chip) + logs_of(2 * chip + 1))
-    mag_ref[...] = jnp.max(allm_ref[:, 0, :channels], axis=0, keepdims=True)
-    mag_out = pltpu.make_async_copy(mag_ref, mag_hbm, store_s.at[2 * chunks])
-    mag_out.start()
+    scale = (jnp.max(allm_ref[:, 0, :channels], axis=0, keepdims=True) + 1e-6) / 127.0
+    scale_ref[...] = scale
+    code_ref[...] = (nk_ref[...].astype(F32) / scale).astype(BF16)
 
     allc_ref[me] = kvc_ref[...]
     alln_ref[me] = kvn_ref[...]
@@ -1230,10 +1227,6 @@
         third = c // 2
         return (1 - c % 2) * even + (c % 2) * (third * odd + (1 - third) * s)
 
-    def y_out(k):
-        here = lanes(k * size, size)
-        return pltpu.make_async_copy(y_ref.at[:, here], y_hbm.at[:, here], store_s.at[k])
-
     def prior(begin, carried):
         here = lanes(begin, size)
         group = begin // (per_group * HEAD_DIM)
@@ -1244,7 +1237,6 @@
     def put_prior(result):
         begin, value = result
         y_ref[:, lanes(begin, size)] = value
-        y_out(begin // size).start()
 
     def rx_wait(slot, j):
         remote(
@@ -1379,8 +1371,6 @@
         return slot(h, 0)
 
     lax.fori_loop(0, steps, second_part, 0)
-    att_out = pltpu.make_async_copy(att_ref, att_hbm, store_s.at[2 * chunks + 1])
-    att_out.start()
     lax.fori_loop(steps, chunks, slot, 0)
     far = order(chunks - 1)
     back_copy(far).wait_recv()
@@ -1409,14 +1399,6 @@
         return 0
 
     lax.fori_loop(0, chunks, drain, 0)
-
-    def stored(k, _):
-        y_out(k).wait()
-        return 0
-
-    lax.fori_loop(0, 2 * chunks, stored, 0)
-    mag_out.wait()
-    att_out.wait()
     for d in range(1, n):
         meta_copy(d).wait_send()
     for way in (1, 2, 0):
@@ -1452,39 +1434,15 @@
             forward(1, chip_).wait_send()
 
 
-def finish_kernel(
-    y_hbm, att_hbm, mag_hbm, nk_hbm, yo_hbm, atto_hbm, code_hbm, scale_ref,
-    y_ref, att_ref, mag_ref, nk_ref, code_ref, in_s, out_s,
-):
-    pieces = 4
-    wide, slim = y_ref.shape[0] // pieces, att_ref.shape[0] // pieces
-    mag_in = pltpu.make_async_copy(mag_hbm, mag_ref, in_s.at[2 * pieces])
-    nk_in = pltpu.make_async_copy(nk_hbm, nk_ref, in_s.at[2 * pieces + 1])
-    code_out = pltpu.make_async_copy(code_ref, code_hbm, out_s.at[2 * pieces])
-    ins, outs = [], []
-    for p in range(pieces):
-        for k, (src, mid, dst, rows) in enumerate(
-            [(y_hbm, y_ref, yo_hbm, wide), (att_hbm, att_ref, atto_hbm, slim)]
-        ):
-            at = pl.ds(p * rows, rows)
-            ins.append(pltpu.make_async_copy(src.at[at], mid.at[at], in_s.at[2 * p + k]))
-            outs.append(pltpu.make_async_copy(mid.at[at], dst.at[at], out_s.at[2 * p + k]))
-    mag_in.start()
-    nk_in.start()
-    for copy in ins:
+def finish_kernel(*refs):
+    count = (len(refs) - 1) // 2
+    copies = [
+        pltpu.make_async_copy(refs[k], refs[count + k], refs[-1].at[k]) for k in range(count)
+    ]
+    for copy in copies:
         copy.start()
-    mag_in.wait()
-    nk_in.wait()
-    scale = (mag_ref[...] + 1e-6) / 127.0
-    scale_ref[...] = scale
-    code_ref[...] = (nk_ref[...].astype(F32) / scale).astype(BF16)
-    code_out.start()
-    for a, b in zip(ins, outs):
-        a.wait()
-        b.start()
-    code_out.wait()
-    for b in outs:
-        b.wait()
+    for copy in copies:
+        copy.wait()
 
 
 def fused_body(
@@ -1520,19 +1478,17 @@
     dma = pltpu.SemaphoreType.DMA
     any_ = pl.BlockSpec(memory_space=pl.ANY)
     piece = pltpu.VMEM((chunks, STATE, size), BF16)
-    y, attended, mag = pl.pallas_call(
+    results = pl.pallas_call(
         functools.partial(fused_kernel, chunks),
         out_shape=(
-            shape((tokens, width), BF16),
-            shape((tokens, q_width), BF16),
-            shape((1, channels), F32),
+            pltpu.VMEM((tokens, width), BF16),
+            pltpu.VMEM((tokens, q_width), BF16),
+            pltpu.VMEM((tokens, channels), BF16),
+            pltpu.VMEM((1, channels), F32),
         ),
         in_specs=[any_] * 14,
-        out_specs=(any_,) * 3,
+        out_specs=(VMEM,) * 4,
         scratch_shapes=[
-            pltpu.VMEM((tokens, width), BF16),
-            pltpu.VMEM((tokens, q_width), BF16),
-            pltpu.VMEM((1, channels), F32),
             pltpu.VMEM((heads, tokens), F32),
             pltpu.VMEM((1, heads), F32),
             pltpu.VMEM((1, tokens), F32),
@@ -1573,7 +1529,6 @@
             pltpu.VMEM((2 * heads, width), BF16),
             pltpu.VMEM((STATE, size), BF16),
             dma((14,)),
-            dma((2 * chunks + 2,)),
             dma((n,)),
             dma((n,)),
             dma((2, 3)),
@@ -1588,7 +1543,7 @@
             dma((chunks,)),
         ],
         compiler_params=pltpu.CompilerParams(
-            collective_id=0, has_side_effects=True, vmem_limit_bytes=60 * 1024 * 1024
+            collective_id=0, has_side_effects=True, vmem_limit_bytes=612 * 1024 * 1024 // 10
         ),
         name="fused",
     )(
@@ -1615,19 +1570,12 @@
             shape((tokens, channels), BF16),
             shape((1, channels), F32),
         ),
-        in_specs=[any_] * 4,
-        out_specs=(any_,) * 3 + (VMEM,),
-        scratch_shapes=[
-            pltpu.VMEM((tokens, width), BF16),
-            pltpu.VMEM((tokens, q_width), BF16),
-            pltpu.VMEM((1, channels), F32),
-            pltpu.VMEM((tokens, channels), BF16),
-            pltpu.VMEM((tokens, channels), BF16),
-            dma((10,)),
-            dma((9,)),
-        ],
+        in_specs=[VMEM] * 4,
+        out_specs=(any_,) * 4,
+        scratch_shapes=[dma((4,))],
+        compiler_params=pltpu.CompilerParams(vmem_limit_bytes=4 * 1024 * 1024),
         name="finish",
-    )(y, attended, mag, new_keys)
+    )(*results)
     return (y, attended, codes, scale.reshape(channels))
 
 

time: 43.8 us -> 41.1 us (0.938)
  Pallas kernels: 42.7 us -> 40.1 us
    pallas_call x1, Pallas kernels: 3.34 us -> 1.56 us  [fused_body(): pl.pallas_call(finish_kernel, out_shape=(shape((tokens, width), BF16), sh...]
    pallas_call x1, Pallas kernels: 39.4 us -> 38.6 us  [fused_body(): pl.pallas_call(functools.partial(fused_kernel, chunks), out_shape=(pltpu....]
where the time goes in v4:
time: 41.1 us; the launch traced here: 40.8 us
  Pallas kernels  40.1 us (98%)
  between operations  0.64 us (2%)
    pallas_call x1, Pallas kernels, fused_body(): pl.pallas_call(functools.partial(fused_kernel, chunks), out_shape=(pltpu....  38.6 us
    pallas_call x1, Pallas kernels, fused_body(): pl.pallas_call(finish_kernel, out_shape=(shape((tokens, width), BF16), sh...  1.56 us

profile of v4, /device:TPU:23, one launch (start us, length us, event | category | flops | bytes accessed | tf_op | source)
XLA Modules:
  0.0 40.8 jit_solution(12819416724181110109)
XLA Ops:
  0.6 38.6 %fused.1 = (bf16[192,4096]{1,0:T(8,128)(2,1)S(1)}, bf16[192,2048]{1,0:T(8,128)(2,1)S(1)}, bf16[192,1024]{1,0:T(8,128)(2,1)S(1)}, f32[1,1024]{1,0:T(1,128)S(1)}) custom-call(bf16[192,4096]{1,0:T(8,128)(2,1)} %x_hbm.1, bf16[192,2048]{1,0:T(8,128)(2,1)} %sin_hbm.1, bf16[192,2048]{1,0:T(8,128)(2,1)} %sout_hbm.1, f32[64,192]{1,0:T(8,128)} %bitcast.7, ...), custom_call_target="tpu_custom_call" | custom-call | tf_op jit(solution)/shard_map/fused/pallas_call | solution.py:1481
  39.2 1.6 %finish.1 = (bf16[192,4096]{1,0:T(8,128)(2,1)}, bf16[192,2048]{1,0:T(8,128)(2,1)}, bf16[192,1024]{1,0:T(8,128)(2,1)}, f32[1,1024]{1,0:T(1,128)}) custom-call(bf16[192,4096]{1,0:T(8,128)(2,1)S(1)} %get-tuple-element.12.refs_0_, bf16[192,2048]{1,0:T(8,128)(2,1)S(1)} %get-tuple-element.13.refs_1_, bf16[192,1024]{1,0:T(8,128)(2,1)S(1)} %get-tuple-element.14.refs_2_, ...), custom_call_target="tpu_custom_call" | custom-call | tf_op jit(solution)/shard_map/finish/pallas_call | solution.py:1565

commit v5 on v4

--- a/solution.py
+++ b/solution.py
@@ -832,6 +832,7 @@
     peak_ref,
     pick_ref,
     carry_ref,
+    wide_ref,
     load_s,
     meta_s,
     meta_r,
@@ -1136,7 +1137,7 @@
     def within(s, _):
         begin = s * 2 * size
         here = lanes(begin, 2 * size)
-        by = spread("z0" if nb > 1 else "out", "skip", begin, 2 * size)
+        by = spread("z0" if nb > 1 else "out", "fade", begin, 2 * size)
         at = 0
         gram = gram_ref[begin // (per_group * HEAD_DIM)]
         x = x_ref[:, here].astype(F32)
@@ -1153,6 +1154,7 @@
             )
         y = by[at : at + tokens] * jnp.concatenate(parts, axis=0)
         y_ref[:, here] = (y + by[at + tokens : at + tokens + 1] * x).astype(BF16)
+        wide_ref[:, here] = by[at + tokens + 16 :].astype(BF16)
         return 0
 
     @pl.when(cx < c)
@@ -1231,7 +1233,7 @@
         here = lanes(begin, size)
         group = begin // (per_group * HEAD_DIM)
         term = jnp.dot(sout_ref[:, lanes(group * STATE, STATE)], carried, preferred_element_type=F32)
-        by = spread("fade", "fade", begin)
+        by = wide_ref[:, here].astype(F32)
         return begin, (y_ref[:, here].astype(F32) + by * term).astype(BF16)
 
     def put_prior(result):
@@ -1277,7 +1279,7 @@
             relay_copy(s).start()
 
     base = 2 + (c // 2) * (4 + c % 2)
-    stride = 1 + (c % 2) * (1 - c // 2)
+    stride = 2 - c // 2
     passes = (c % 2) * near + (1 - c % 2) * (chunks - near)
 
     def pass_at(place):
@@ -1342,11 +1344,12 @@
     pass_at(2)
 
     def first_part(h, _):
-        attend_cache(h, streams, together, q_ref, allc_ref, sum_ref, peak_ref)
-        pass_at(3 + h)
+        attend_cache(h, streams, 2 * together, q_ref, allc_ref, sum_ref, peak_ref)
+        pass_at(3 + 2 * h)
+        pass_at(4 + 2 * h)
         return 0
 
-    lax.fori_loop(0, steps, first_part, 0)
+    lax.fori_loop(0, steps // 2, first_part, 0)
     span_arrived()
 
     def second_part(h, _):
@@ -1528,6 +1531,7 @@
             pltpu.VMEM((q_width // ATT_DIM * tokens, 128), F32),
             pltpu.VMEM((2 * heads, width), BF16),
             pltpu.VMEM((STATE, size), BF16),
+            pltpu.VMEM((tokens, width), BF16),
             dma((14,)),
             dma((n,)),
             dma((n,)),

time: 41.1 us -> 40.5 us (0.985)
    pallas_call x1, Pallas kernels: 38.6 us -> 38.1 us  [fused_body(): pl.pallas_call(functools.partial(fused_kernel, chunks), out_shape=(pltpu....]
where the time goes in v5:
time: 40.5 us; the launch traced here: 40.3 us
  Pallas kernels  39.7 us (98%)
  between operations  0.64 us (2%)
    pallas_call x1, Pallas kernels, fused_body(): pl.pallas_call(functools.partial(fused_kernel, chunks), out_shape=(pltpu....  38.1 us
    pallas_call x1, Pallas kernels, fused_body(): pl.pallas_call(finish_kernel, out_shape=(shape((tokens, width), BF16), sh...  1.56 us

profile of v5, /device:TPU:23, one launch (start us, length us, event | category | flops | bytes accessed | tf_op | source)
XLA Modules:
  0.0 40.3 jit_solution(369995835653179858)
XLA Ops:
  0.6 38.1 %fused.1 = (bf16[192,4096]{1,0:T(8,128)(2,1)S(1)}, bf16[192,2048]{1,0:T(8,128)(2,1)S(1)}, bf16[192,1024]{1,0:T(8,128)(2,1)S(1)}, f32[1,1024]{1,0:T(1,128)S(1)}) custom-call(bf16[192,4096]{1,0:T(8,128)(2,1)} %x_hbm.1, bf16[192,2048]{1,0:T(8,128)(2,1)} %sin_hbm.1, bf16[192,2048]{1,0:T(8,128)(2,1)} %sout_hbm.1, f32[64,192]{1,0:T(8,128)} %bitcast.7, ...), custom_call_target="tpu_custom_call" | custom-call | tf_op jit(solution)/shard_map/fused/pallas_call | solution.py:1484
  38.8 1.6 %finish.1 = (bf16[192,4096]{1,0:T(8,128)(2,1)}, bf16[192,2048]{1,0:T(8,128)(2,1)}, bf16[192,1024]{1,0:T(8,128)(2,1)}, f32[1,1024]{1,0:T(1,128)}) custom-call(bf16[192,4096]{1,0:T(8,128)(2,1)S(1)} %get-tuple-element.12.refs_0_, bf16[192,2048]{1,0:T(8,128)(2,1)S(1)} %get-tuple-element.13.refs_1_, bf16[192,1024]{1,0:T(8,128)(2,1)S(1)} %get-tuple-element.14.refs_2_, ...), custom_call_target="tpu_custom_call" | custom-call | tf_op jit(solution)/shard_map/finish/pallas_call | solution.py:1569

commit v6 on v5

--- a/solution.py
+++ b/solution.py
@@ -1360,7 +1360,7 @@
                 attend_span(
                     h,
                     streams,
-                    together,
+                    2 * together,
                     chip,
                     q_ref,
                     alln_ref,
@@ -1370,10 +1370,12 @@
                     att_ref,
                 )
 
-        pass_at(3 + steps + h)
-        return slot(h, 0)
-
-    lax.fori_loop(0, steps, second_part, 0)
+        for e in range(2):
+            pass_at(3 + steps + 2 * h + e)
+            slot(2 * h + e, 0)
+        return 0
+
+    lax.fori_loop(0, steps // 2, second_part, 0)
     lax.fori_loop(steps, chunks, slot, 0)
     far = order(chunks - 1)
     back_copy(far).wait_recv()

time: 40.5 us -> 41.9 us (1.035)
  Pallas kernels: 39.7 us -> 40.9 us
    pallas_call x1, Pallas kernels: 38.1 us -> 39.4 us  [fused_body(): pl.pallas_call(functools.partial(fused_kernel, chunks), out_shape=(pltpu....]
where the time goes in v6:
time: 41.9 us; the launch traced here: 41.7 us
  Pallas kernels  40.9 us (98%)
  between operations  0.81 us (2%)
    pallas_call x1, Pallas kernels, fused_body(): pl.pallas_call(functools.partial(fused_kernel, chunks), out_shape=(pltpu....  39.4 us
    pallas_call x1, Pallas kernels, fused_body(): pl.pallas_call(finish_kernel, out_shape=(shape((tokens, width), BF16), sh...  1.56 us

profile of v6, /device:TPU:23, one launch (start us, length us, event | category | flops | bytes accessed | tf_op | source)
XLA Modules:
  0.0 41.7 jit_solution(3305946774742617814)
XLA Ops:
  0.6 39.4 %fused.1 = (bf16[192,4096]{1,0:T(8,128)(2,1)S(1)}, bf16[192,2048]{1,0:T(8,128)(2,1)S(1)}, bf16[192,1024]{1,0:T(8,128)(2,1)S(1)}, f32[1,1024]{1,0:T(1,128)S(1)}) custom-call(bf16[192,4096]{1,0:T(8,128)(2,1)} %x_hbm.1, bf16[192,2048]{1,0:T(8,128)(2,1)} %sin_hbm.1, bf16[192,2048]{1,0:T(8,128)(2,1)} %sout_hbm.1, f32[64,192]{1,0:T(8,128)} %bitcast.7, ...), custom_call_target="tpu_custom_call" | custom-call | tf_op jit(solution)/shard_map/fused/pallas_call | solution.py:1486
  40.0 1.6 %finish.1 = (bf16[192,4096]{1,0:T(8,128)(2,1)}, bf16[192,2048]{1,0:T(8,128)(2,1)}, bf16[192,1024]{1,0:T(8,128)(2,1)}, f32[1,1024]{1,0:T(1,128)}) custom-call(bf16[192,4096]{1,0:T(8,128)(2,1)S(1)} %get-tuple-element.12.refs_0_, bf16[192,2048]{1,0:T(8,128)(2,1)S(1)} %get-tuple-element.13.refs_1_, bf16[192,1024]{1,0:T(8,128)(2,1)S(1)} %get-tuple-element.14.refs_2_, ...), custom_call_target="tpu_custom_call" | custom-call | tf_op jit(solution)/shard_map/finish/pallas_call | solution.py:1571
